TPU v7x, 128 devices: a whole 4x4x4 slice. The times are simulated.
128 devices in a mesh: clients: 16 (over x, y_hi, core), shard: 8 (over z, y_lo).
Axes of the slice: x: 4, y: 4 (y_hi: 2, y_lo: 2; y = y_hi * 2 + y_lo), z: 4, core: 2. Of those that a mesh axis runs over, the one named last changes fastest.
Arguments:
- client_deltas: bfloat16 [256, 128, 3584], P(('clients', 'shard')), may hold values from -24 to 24
- variate_deltas: bfloat16 [256, 128, 3584], P(('clients', 'shard')), may hold values from -6 to 6
- params: float32 [128, 3584], P(('clients', 'shard')), may hold values from -1.5 to 1.5
- variate: float32 [128, 3584], P(('clients', 'shard')), may hold values from -1.5 to 1.5
- taking_part: int32 [256], P(('clients', 'shard')), may hold values from 0 to 1, as said below
- counts: int32 [256], P(('clients', 'shard')), may hold values from 32 to 287
Outputs:
- new_params: float32 [128, 3584], P(('clients', 'shard'))
- new_variate: float32 [128, 3584], P(('clients', 'shard'))
- client_params: bfloat16 [128, 3584], replicated
- client_variate: bfloat16 [128, 3584], replicated
Inputs may be any that keep to these rules, and one draw needn't show every extreme that they name: `taking_part`: at least one client takes part.
All inputs are finite; a program needn't handle non-finite values.
Results may differ from a plain program's by a relative error of at most 0.001.
Values may be sent and summed in bfloat16 or wider, within the bound.
No kernel may reach another device: no remote copies, remote signals or barrier semaphores. Data moves between devices by JAX's collectives and lax.ppermute only.
A program may use at most 64 MiB of HBM per device.

v0:
```python
import jax
import jax.numpy as jnp
from jax import lax
from jax.sharding import PartitionSpec as P


def in_order(parts, dim):
    parts = jnp.moveaxis(parts, 0, dim)
    dims = parts.shape
    return parts.reshape(*dims[:dim], dims[dim] * dims[dim + 1], *dims[dim + 2 :])


def gather_together(arrays, axis, dims):
    ravelled = jnp.concatenate([a.reshape(-1) for a in arrays])
    lines, at, finished = (lax.all_gather(ravelled, axis), 0, [])
    for a, dim in zip(arrays, dims):
        parts = lines[:, at : at + a.size].reshape(-1, *a.shape)
        finished.append(in_order(parts, dim))
        at += a.size
    return tuple(finished)


def in_blocks(x, dim, count):
    dims = x.shape
    parts = x.reshape(*dims[:dim], count, dims[dim] // count, *dims[dim + 1 :])
    return jnp.moveaxis(parts, dim, 0)


def one_scatter(arrays, axis, dims):
    count = lax.axis_size(axis)
    parts = [in_blocks(a, dim, count) for a, dim in zip(arrays, dims)]
    lines = jnp.concatenate([b.reshape(count, -1) for b in parts], axis=1)
    width = max(16, -(-lines.shape[1] // 1024) * 8)
    lines = jnp.pad(lines, ((0, 0), (0, width * 128 - lines.shape[1]))).reshape(-1, 128)
    ravelled, at, finished = (lax.psum_scatter(lines, axis, tiled=True).reshape(-1), 0, [])
    for b in parts:
        part = b[0]
        finished.append(ravelled[at : at + part.size].reshape(part.shape))
        at += part.size
    return tuple(finished)


def in_one_piece(arrays, axis, dim, along):
    widths = [a.shape[along] for a in arrays]
    both = jnp.concatenate(arrays, axis=along)
    result = lax.all_gather(both, axis, axis=dim, tiled=True)
    return tuple(jnp.split(result, [sum(widths[:k]) for k in range(1, len(widths))], axis=along))


def weight_rows(taking_part, counts):
    weight = taking_part * counts
    upper_part = weight // 16 * 16
    lower_part = weight - upper_part
    weight_table = jnp.stack([upper_part, lower_part]).astype(jnp.bfloat16)
    chosen = taking_part.astype(jnp.bfloat16)[None, :]
    return (weight_table, chosen, jnp.sum(weight).astype(jnp.float32))


def weigh_blocks(weight_table, chosen, deltas, changes):
    client_count = deltas.shape[0]
    local_rows = deltas.shape[1]
    columns = deltas.shape[2]
    moved_sum = jnp.dot(
        weight_table, deltas.reshape(client_count, -1), preferred_element_type=jnp.float32
    )
    varied = jnp.dot(chosen, changes.reshape(client_count, -1), preferred_element_type=jnp.float32)
    return (
        (moved_sum[0] + moved_sum[1]).reshape(local_rows, columns),
        varied.reshape(local_rows, columns),
    )


def body(client_deltas, variate_deltas, params, variate, taking_part, counts):
    all_part, all_counts = gather_together((taking_part, counts), ("clients", "shard"), (0, 0))
    weight_table, chosen, weight_total = weight_rows(all_part, all_counts)
    client_count = all_part.shape[0]
    own_table, own_chosen, unused_total = weight_rows(taking_part, counts)
    own_sum, own_shift = weigh_blocks(own_table, own_chosen, client_deltas, variate_deltas)
    summed, shifted = one_scatter((own_sum, own_shift), ("clients", "shard"), (0, 0))
    new_params = params + summed / weight_total
    new_variate = variate + shifted / jnp.float32(client_count)
    client_params, client_variate = in_one_piece(
        (new_params.astype(jnp.bfloat16), new_variate.astype(jnp.bfloat16)),
        ("clients", "shard"),
        0,
        1,
    )
    return (new_params, new_variate, client_params, client_variate)


def solution(mesh):
    in_specs = (
        P(("clients", "shard"), None, None),
        P(("clients", "shard"), None, None),
        P(("clients", "shard"), None),
        P(("clients", "shard"), None),
        P(("clients", "shard")),
        P(("clients", "shard")),
    )
    out_specs = (P(("clients", "shard"), None), P(("clients", "shard"), None), P(), P())
    return jax.shard_map(body, mesh=mesh, in_specs=in_specs, out_specs=out_specs, check_vma=False)
```

profile of v0, /device:TPU:1, one launch (start us, length us, event | category | flops | bytes accessed | tf_op | source)
XLA Modules:
  0.0 515.3 jit_solution(6312435250725367843)
XLA Ops:
  7.2 0.0 all-reduce.4.cloned.1.call-start
  7.2 0.7 convert_bitcast_fusion.2
  7.9 0.7 convert_bitcast_fusion.1
  8.6 3.4 copy.13
  12.0 2.0 fusion.5
  14.0 16.5 %fusion = f32[458752]{0:T(1024)} fusion(f32[2,458752]{1,0:T(2,128)S(1)} %fusion.5), kind=kLoop, calls=%fused_computation.2 | loop fusion | flops 458752 | bytes 5505024 | tf_op jit(solution)/shard_map/add | solution.py:68
  30.5 0.0 copy-start.2
  30.5 1.6 add.17
  32.1 0.0 copy-done.2
  32.1 3.6 fusion.6
  35.7 0.1 copy.26
  35.8 2.1 pad_maximum_fusion
  37.9 4.9 reshape.64
  42.8 0.0 copy-start.3
  42.8 0.0 copy-start
  42.8 0.0 copy-start.1
  42.8 0.0 all-reduce.4.cloned.1.call-update
  42.8 0.0 all-gather.4.cloned.1.call-start
  42.9 0.6 copy-done.3
  43.4 0.2 add_dynamic-update-slice_fusion
  43.6 69.0 %all-reduce = s32[512]{0:T(512)S(1)} all-reduce(s32[512]{0:T(512)S(1)} %add_dynamic-update-slice_fusion), channel_id=2, replica_groups=mesh['clients'=16,'shard'=8] {'clients','shard'}, use_global_device_ids=true, to_apply=%add | all-reduce | flops 512 | bytes 4096
  112.6 0.1 reshape.65
  112.7 0.7 fusion.1
  114.1 85.6 %all-reduce.4.cloned.1.call-done = f32[7168,128]{1,0:T(8,128)} async-done(((f32[7168,128]{1,0:T(8,128)}), f32[7168,128]{1,0:T(8,128)}) %all-reduce.4.cloned.1.call-update) | async-done | bytes 3670032
  199.7 0.8 fusion.2
  200.5 0.0 copy-done
  200.5 0.0 copy-done.1
  200.5 0.7 fusion.8
  201.2 0.6 maximum_bitcast_fusion
  201.8 0.0 all-gather.4.cloned.1.call-update
  201.8 302.7 %all-gather.4.cloned.1.call-done = bf16[128,1,7168]{2,1,0:T(2,128)(2,1)} async-done(((bf16[1,1,7168]{2,1,0:T(2,128)(2,1)}), bf16[128,1,7168]{2,1,0:T(2,128)(2,1)}) %all-gather.4.cloned.1.call-update) | async-done | bytes 1835024 | tf_op jit(solution)/shard_map/all_gather | solution.py:46
  504.5 2.6 copy.25
  507.1 1.3 fusion.11
  (1 shorter events, 0.0 us)
Async XLA Ops:
  7.2 192.5 %all-reduce.4.cloned.1.call-start = ((), (), s32[]{:S(2)}) async-start(), calls=%async_computation.1 | async-start | bytes 7340032
  30.5 1.6 copy-start.2
  42.8 0.7 copy-start.3
  42.8 157.7 %copy-start = (f32[1,3584]{1,0:T(1,128)S(1)}, f32[1,3584]{1,0:T(1,128)}, u32[]{:S(2)}) copy-start(f32[1,3584]{1,0:T(1,128)} %param.8) | copy-start | bytes 43012
  42.8 157.7 %copy-start.1 = (f32[1,3584]{1,0:T(1,128)S(1)}, f32[1,3584]{1,0:T(1,128)}, u32[]{:S(2)}) copy-start(f32[1,3584]{1,0:T(1,128)} %param.9) | copy-start | bytes 43012
  42.8 461.7 %all-gather.4.cloned.1.call-start = ((), (), s32[]{:S(2)}) async-start(), calls=%async_computation | async-start | bytes 3698688 | tf_op jit(solution)/shard_map/all_gather | solution.py:46
Sparse Core Ops, SparseCore 0:
  42.9 156.7 all-reduce.3
  202.0 302.4 all-gather.3
where the time goes:
time: 516 us; the launch traced here: 515 us
  waiting for transfers between devices  388 us (75%)
  blocking collectives  69 us (13%)
  other arithmetic  22.9 us (4%)
  between operations  14.8 us (3%)
  local copies, waits for them, and re-layouts  14.6 us (3%)
  matrix products  5.62 us (1%)
    all_gather x1, waiting for transfers between devices, in_one_piece(): result = lax.all_gather(both, axis, axis=dim, tiled=True)  303 us
    unnamed x3, waiting for transfers between devices  85.7 us
    unnamed x1, blocking collectives  69 us
    add x1, other arithmetic, weigh_blocks(): moved_sum[0] + moved_sum[1]  16.5 us
  transfers between devices with their start and end apart: 2, of which 2 were waited for; matrix products, arithmetic and copies ran while one was open for 0% of the time, Pallas kernels for 0%

commit v1 on v0

v1 whole, which is shorter than its diff:
```python
import functools

import jax
import jax.numpy as jnp
from jax import lax
from jax.experimental import pallas as pl
from jax.experimental.pallas import tpu as pltpu
from jax.sharding import Mesh
from jax.sharding import PartitionSpec as P

FINE = (("x", 4), ("yh", 2), ("core", 2), ("z", 4), ("yl", 2))
ALL = ("x", "yh", "core", "z", "yl")
CHIPS = ("x", "yh", "z", "yl")
N_CHIPS = 64
LANES = 128


def core_swap(x):
    return lax.ppermute(x, "core", [(0, 1), (1, 0)])


def weigh_kernel(scalars, deltas, changes, keep, send):
    core = scalars[0]
    w0 = scalars[1].astype(jnp.float32)
    w1 = scalars[2].astype(jnp.float32)
    t0 = scalars[3].astype(jnp.float32)
    t1 = scalars[4].astype(jnp.float32)
    pieces = deltas.shape[2] // LANES
    per_block = keep.shape[0] // 8

    def fill(out, source, a0, a1, tail):
        for half in range(2):
            rows = pl.ds(half * 8, 8)
            for j in range(pieces):
                lanes = pl.ds(j * LANES, LANES)
                value = source[0, rows, lanes].astype(jnp.float32) * a0
                value = value + source[1, rows, lanes].astype(jnp.float32) * a1
                out[pl.ds(half * pieces + j, 8, stride=per_block), :] = value
        for block in range(8):
            out[pl.ds(block * per_block + 2 * pieces, 8), :] = jnp.full((8, LANES), tail)

    @pl.when(core == 0)
    def _():
        fill(keep, deltas, w0, w1, w0 + w1)
        fill(send, changes, t0, t1, 0.0)

    @pl.when(core == 1)
    def _():
        fill(send, deltas, w0, w1, w0 + w1)
        fill(keep, changes, t0, t1, 0.0)


def weigh(scalars, deltas, changes):
    rows, columns = deltas.shape[1:]
    per_block = 2 * columns // LANES + 8
    in_spec = pl.BlockSpec((2, 16, columns), lambda i, s: (0, i, 0))
    out_spec = pl.BlockSpec((8 * per_block, LANES), lambda i, s: (i, 0))
    out = jax.ShapeDtypeStruct((rows // 16 * 8 * per_block, LANES), jnp.float32)
    return pl.pallas_call(
        weigh_kernel,
        grid_spec=pltpu.PrefetchScalarGridSpec(
            num_scalar_prefetch=1,
            grid=(rows // 16,),
            in_specs=[in_spec, in_spec],
            out_specs=[out_spec, out_spec],
        ),
        out_shape=[out, out],
        name="weigh",
    )(scalars, deltas, changes)


def update_kernel(client_count, core_ref, blocks, base, new, rounded):
    total = blocks[0]
    for k in range(1, blocks.shape[0]):
        total = total + blocks[k]
    used = base.shape[0]
    weight = jnp.broadcast_to(total[used : used + 1], (1, LANES))
    divisor = jnp.where(core_ref[0] == 0, weight, jnp.float32(client_count))
    fresh = base[...] + total[:used] / divisor
    new[...] = fresh
    rounded[...] = fresh.astype(jnp.bfloat16)


def update(core, blocks, base, client_count):
    vmem = pl.BlockSpec(memory_space=pltpu.VMEM)
    return pl.pallas_call(
        functools.partial(update_kernel, client_count),
        in_specs=[pl.BlockSpec(memory_space=pltpu.SMEM), vmem, vmem],
        out_specs=[vmem, vmem],
        out_shape=[
            jax.ShapeDtypeStruct(base.shape, jnp.float32),
            jax.ShapeDtypeStruct(base.shape, jnp.bfloat16),
        ],
        name="update",
    )(core, blocks, base)


def to_rows(gathered):
    parts = gathered.reshape(8, 8, 2, -1)
    return jnp.transpose(parts, (0, 2, 1, 3)).reshape(128, -1)


def body(client_deltas, variate_deltas, params, variate, taking_part, counts):
    core = lax.axis_index("core").astype(jnp.int32)
    first = core == 0
    weight = taking_part * counts
    client_count = 2 * 128
    pieces = params.shape[1] // LANES

    scalars = jnp.concatenate([core[None], weight, taking_part])
    keep, send = weigh(scalars, client_deltas, variate_deltas)

    own_base = jnp.where(first, params, variate)
    other_base = core_swap(jnp.where(first, variate, params))
    base = jnp.concatenate(
        [jnp.where(first, own_base, other_base), jnp.where(first, other_base, own_base)]
    ).reshape(2 * pieces, LANES)

    both = (keep + core_swap(send)).reshape(N_CHIPS, -1, LANES)
    blocks = lax.all_to_all(both, CHIPS, 0, 0, tiled=True)
    new, rounded = update(core[None], blocks, base, client_count)

    new = new.reshape(2, -1)
    other_new = core_swap(jnp.where(first, new[1:], new[:1]))
    own_new = jnp.where(first, new[:1], new[1:])
    new_params = jnp.where(first, own_new, other_new)
    new_variate = jnp.where(first, other_new, own_new)

    spread = jnp.broadcast_to(rounded[None], (N_CHIPS, *rounded.shape))
    gathered = lax.all_to_all(spread, CHIPS, 0, 0, tiled=True)
    swapped = core_swap(gathered)
    own_rows = to_rows(gathered)
    other_rows = to_rows(swapped)
    client_params = jnp.where(first, own_rows, other_rows)
    client_variate = jnp.where(first, other_rows, own_rows)
    return (new_params, new_variate, client_params, client_variate)


def solution(mesh):
    fine = Mesh(mesh.devices.reshape([n for _, n in FINE]), [a for a, _ in FINE])
    in_specs = (
        P(ALL, None, None),
        P(ALL, None, None),
        P(ALL, None),
        P(ALL, None),
        P(ALL),
        P(ALL),
    )
    out_specs = (P(ALL, None), P(ALL, None), P(), P())
    return jax.shard_map(body, mesh=fine, in_specs=in_specs, out_specs=out_specs, check_vma=False)
```

time: 516 us -> 95 us (0.18)
  waiting for transfers between devices: 388 us -> 33.5 us
  blocking collectives: 69 us -> 23 us
  other arithmetic: 22.9 us -> 5.87 us
  starting transfers between devices: 0.08 us -> 15.5 us
  between operations: 14.8 us -> 0.73 us
  Pallas kernels: 0 us -> 10.6 us
  local copies, waits for them, and re-layouts: 14.6 us -> 5.31 us
  matrix products: 5.62 us -> 0 us
    all_gather x1 -> x0, waiting for transfers between devices: 303 us -> none  [in_one_piece(): result = lax.all_gather(both, axis, axis=dim, tiled=True)]
    unnamed x3 -> x0, waiting for transfers between devices: 85.7 us -> none
    unnamed x1 -> x0, blocking collectives: 69 us -> none
    all_to_all x0 -> x1, waiting for transfers between devices: none -> 26.6 us  [body(): blocks = lax.all_to_all(both, CHIPS, 0, 0, tiled=True)]
    all_to_all x0 -> x1, blocking collectives: none -> 23 us  [body(): gathered = lax.all_to_all(spread, CHIPS, 0, 0, tiled=True)]
    add x1, other arithmetic: 16.5 us -> 3.12 us  [body(): both = (keep + core_swap(send)).reshape(N_CHIPS, -1, LANES)]
    all_to_all x0 -> x1, starting transfers between devices: none -> 11.4 us  [body(): blocks = lax.all_to_all(both, CHIPS, 0, 0, tiled=True)]
    pallas_call x0 -> x2, Pallas kernels: none -> 10.6 us  [the longest x1 8.23 us: weigh(): pl.pallas_call(weigh_kernel, grid_spec=pltpu.PrefetchScalarGridSpec(num_s...]
  transfers between devices with their start and end apart: 2 -> 5, of which waited for: 2 -> 4; matrix products, arithmetic and copies ran while one was open for 0% -> 1% of each run, Pallas kernels for 0% -> 0%
where the time goes in v1:
time: 95 us; the launch traced here: 94.4 us
  waiting for transfers between devices  33.5 us (35%)
  blocking collectives  23 us (24%)
  starting transfers between devices  15.5 us (16%)
  Pallas kernels  10.6 us (11%)
  other arithmetic  5.87 us (6%)
  local copies, waits for them, and re-layouts  5.31 us (6%)
    all_to_all x1, waiting for transfers between devices, body(): blocks = lax.all_to_all(both, CHIPS, 0, 0, tiled=True)  26.6 us
    all_to_all x1, blocking collectives, body(): gathered = lax.all_to_all(spread, CHIPS, 0, 0, tiled=True)  23 us
    all_to_all x1, starting transfers between devices, body(): blocks = lax.all_to_all(both, CHIPS, 0, 0, tiled=True)  11.4 us
    pallas_call x1, Pallas kernels, weigh(): pl.pallas_call(weigh_kernel, grid_spec=pltpu.PrefetchScalarGridSpec(num_s...  8.23 us
    ppermute x4, waiting for transfers between devices, core_swap(): return lax.ppermute(x, 'core', [(0, 1), (1, 0)])  6.83 us
    ppermute x4, starting transfers between devices, core_swap(): return lax.ppermute(x, 'core', [(0, 1), (1, 0)])  4.13 us
    add x1, other arithmetic, body(): both = (keep + core_swap(send)).reshape(N_CHIPS, -1, LANES)  3.12 us
    pallas_call x1, Pallas kernels, update(): pl.pallas_call(functools.partial(update_kernel, client_count), in_specs=[...  2.35 us
  transfers between devices with their start and end apart: 5, of which 4 were waited for; matrix products, arithmetic and copies ran while one was open for 1% of the time, Pallas kernels for 0%

profile of v1, /device:TPU:1, one launch (start us, length us, event | category | flops | bytes accessed | tf_op | source)
XLA Modules:
  0.0 94.4 jit_solution(1974209908236289038)
XLA Ops:
  0.6 0.7 mul.3
  1.3 1.2 %pad_add_fusion.scalars = s32[5]{0:T(128)} fusion(s32[2]{0:T(128)} %param.10, s32[2]{0:T(128)S(1)} %mul.3, s32[1]{0:T(128)} %bitcast.core_ref), kind=kLoop, calls=%fused_computation.12 | loop fusion | flops 10 | bytes 40 | tf_op jit(solution)/shard_map/concatenate | solution.py:110
  2.6 8.2 %weigh.1 = (f32[4096,128]{1,0:T(8,128)}, f32[4096,128]{1,0:T(8,128)}) custom-call(s32[5]{0:T(128)} %pad_add_fusion.scalars, bf16[2,128,3584]{2,1,0:T(8,128)(2,1)} %deltas.1, bf16[2,128,3584]{2,1,0:T(8,128)(2,1)} %changes.1), custom_call_target="tpu_custom_call" | custom-call | tf_op jit(solution)/shard_map/weigh/pallas_call | solution.py:59
  10.8 1.4 %collective-permute-start = (f32[4096,128]{1,0:T(8,128)}, f32[4096,128]{1,0:T(8,128)S(1)}, u32[]{:S(2)}, u32[]{:S(2)}) collective-permute-start(f32[4096,128]{1,0:T(8,128)} %get-tuple-element.9), channel_id=1, source_target_pairs={{0,8},{8,0},{1,9},{9,1},{2,10},{10,2},{3,11},{11,3},{4,12},{12,4},... | collective-permute-start | bytes 6291464 | tf_op jit(solution)/shard_map/ppermute | solution.py:19
  12.2 4.0 %collective-permute-done = f32[4096,128]{1,0:T(8,128)S(1)} collective-permute-done((f32[4096,128]{1,0:T(8,128)}, f32[4096,128]{1,0:T(8,128)S(1)}, u32[]{:S(2)}, u32[]{:S(2)}) %collective-permute-start) | collective-permute-done | bytes 2097184 | tf_op jit(solution)/shard_map/ppermute | solution.py:19
  16.2 3.1 %add.3 = f32[4096,128]{1,0:T(8,128)} add(f32[4096,128]{1,0:T(8,128)} %get-tuple-element.8, f32[4096,128]{1,0:T(8,128)S(1)} %collective-permute-done) | non-fusion elementwise | flops 524288 | bytes 6291456 | tf_op jit(solution)/shard_map/add | solution.py:119
  19.3 0.0 copy-start.1
  19.3 0.0 copy-start.2
  19.3 11.4 %all-to-all-start = ((f32[64,64,128]{2,1,0:T(8,128)}), f32[64,64,128]{2,1,0:T(8,128)S(1)}, u32[]{:S(2)}, u32[]{:S(2)}) async-start(f32[64,64,128]{2,1,0:T(8,128)} %bitcast.1), calls=%async_computation | async-start | bytes 4194304 | tf_op jit(solution)/shard_map/all_to_all | solution.py:120
  30.7 0.0 copy-done.1
  30.7 0.0 copy-done.2
  30.7 0.7 collective-permute-start.1
  31.4 0.8 collective-permute-done.1
  32.4 0.6 reshape.75.base
  33.0 26.6 %all-to-all-done.blocks = f32[64,64,128]{2,1,0:T(8,128)S(1)} async-done(((f32[64,64,128]{2,1,0:T(8,128)}), f32[64,64,128]{2,1,0:T(8,128)S(1)}, u32[]{:S(2)}, u32[]{:S(2)}) %all-to-all-start) | async-done | bytes 2097184 | tf_op jit(solution)/shard_map/all_to_all | solution.py:120
  59.6 0.0 copy-start
  59.6 1.3 %copy-done = f32[64,64,128]{2,1,0:T(8,128)} copy-done((f32[64,64,128]{2,1,0:T(8,128)}, f32[64,64,128]{2,1,0:T(8,128)S(1)}, u32[]{:S(2)}) %copy-start) | copy-done | bytes 2097176
  61.0 2.3 %update.1 = (f32[56,128]{1,0:T(8,128)}, bf16[56,128]{1,0:T(8,128)(2,1)}) custom-call(s32[1]{0:T(128)} %bitcast.core_ref, f32[64,64,128]{2,1,0:T(8,128)} %copy-done, f32[56,128]{1,0:T(8,128)} %reshape.75.base), custom_call_target="tpu_custom_call" | custom-call | tf_op jit(solution)/shard_map/update/pallas_call | solution.py:86
  63.3 0.0 copy-start.3
  63.3 0.8 broadcast_in_dim.5
  64.1 23.0 %all_to_all.10 = bf16[64,56,128]{2,1,0:T(8,128)(2,1)S(1)} all-to-all(bf16[64,56,128]{2,1,0:T(8,128)(2,1)S(1)} %broadcast_in_dim.5), channel_id=1, replica_groups=mesh['x'=4,'yh'=2,'core'=2,'z'=4,'yl'=2] {'x','yh','z','yl'}, dimensions={0} | all-to-all | bytes 1835008 | tf_op jit(solution)/shard_map/all_to_all | solution.py:130
  87.1 1.9 %collective-permute-start.3 = (bf16[64,56,128]{2,1,0:T(8,128)(2,1)S(1)}, bf16[64,56,128]{2,1,0:T(8,128)(2,1)S(1)}, u32[]{:S(2)}, u32[]{:S(2)}) collective-permute-start(bf16[64,56,128]{2,1,0:T(8,128)(2,1)S(1)} %all_to_all.10), channel_id=1, source_target_pairs={{0,8},{8,0},{1,9},{9,1},{2,10},{10,2},{3,11},{11,3},{4,12},{12,4},... | collective-permute-start | bytes 2752520 | tf_op jit(solution)/shard_map/ppermute | solution.py:19
  89.0 0.0 copy-done.3
  89.1 0.1 collective-permute-start.2
  89.2 2.0 %collective-permute-done.2 = f32[1,3584]{1,0:T(1,128)S(1)} collective-permute-done((f32[1,3584]{1,0:T(1,128)S(1)}, f32[1,3584]{1,0:T(1,128)S(1)}, u32[]{:S(2)}, u32[]{:S(2)}) %collective-permute-start.2) | collective-permute-done | bytes 14368 | tf_op jit(solution)/shard_map/ppermute | solution.py:19
  91.2 0.6 broadcast_select_fusion.2
  91.8 0.0 collective-permute-done.3
  91.8 0.1 broadcast_select_fusion
  91.9 0.2 select_n.104
  92.2 1.0 %copy.10 = bf16[8,2,8,3584]{3,2,1,0:T(8,128)(2,1)} copy(bf16[8,2,8,3584]{3,1,2,0:T(2,128)(2,1)S(1)} %bitcast.18) | data formatting | bytes 1835008 | tf_op jit(solution)/shard_map/jit(_where)/select_n | solution.py:134
  93.2 0.2 select_n.108
  93.4 1.0 %copy.11 = bf16[8,2,8,3584]{3,2,1,0:T(8,128)(2,1)} copy(bf16[8,2,8,3584]{3,1,2,0:T(2,128)(2,1)S(1)} %bitcast.19) | data formatting | bytes 1835008 | tf_op jit(solution)/shard_map/jit(_where)/select_n | solution.py:135
  (5 shorter events, 0.1 us)
Async XLA Ops:
  10.8 5.4 %collective-permute-start = (f32[4096,128]{1,0:T(8,128)}, f32[4096,128]{1,0:T(8,128)S(1)}, u32[]{:S(2)}, u32[]{:S(2)}) collective-permute-start(f32[4096,128]{1,0:T(8,128)} %get-tuple-element.9), channel_id=1, source_target_pairs={{0,8},{8,0},{1,9},{9,1},{2,10},{10,2},{3,11},{11,3},{4,12},{12,4},... | collective-permute-start | bytes 6291464 | tf_op jit(solution)/shard_map/ppermute | solution.py:19
  19.3 11.4 %copy-start.1 = (f32[1,3584]{1,0:T(1,128)S(1)}, f32[1,3584]{1,0:T(1,128)}, u32[]{:S(2)}) copy-start(f32[1,3584]{1,0:T(1,128)} %param.9) | copy-start | bytes 43012
  19.3 11.4 %copy-start.2 = (f32[1,3584]{1,0:T(1,128)S(1)}, f32[1,3584]{1,0:T(1,128)}, u32[]{:S(2)}) copy-start(f32[1,3584]{1,0:T(1,128)} %param.8) | copy-start | bytes 43012
  19.3 40.3 %all-to-all-start = ((f32[64,64,128]{2,1,0:T(8,128)}), f32[64,64,128]{2,1,0:T(8,128)S(1)}, u32[]{:S(2)}, u32[]{:S(2)}) async-start(f32[64,64,128]{2,1,0:T(8,128)} %bitcast.1), calls=%async_computation | async-start | bytes 4194304 | tf_op jit(solution)/shard_map/all_to_all | solution.py:120
  30.7 1.6 %collective-permute-start.1 = (f32[1,3584]{1,0:T(1,128)S(1)}, f32[1,3584]{1,0:T(1,128)S(1)}, u32[]{:S(2)}, u32[]{:S(2)}) collective-permute-start(f32[1,3584]{1,0:T(1,128)S(1)} %broadcast_select_fusion.6), channel_id=1, source_target_pairs={{0,8},{8,0},{1,9},{9,1},{2,10},{10,2},{3,11},{11,3},{4,12},{12,4},... | collective-permute-start | bytes 43016 | tf_op jit(solution)/shard_map/ppermute | solution.py:19
  59.6 1.3 %copy-start = (f32[64,64,128]{2,1,0:T(8,128)}, f32[64,64,128]{2,1,0:T(8,128)S(1)}, u32[]{:S(2)}) copy-start(f32[64,64,128]{2,1,0:T(8,128)S(1)} %all-to-all-done.blocks) | copy-start | bytes 6291460
  63.3 25.7 %copy-start.3 = (f32[56,128]{1,0:T(8,128)S(1)}, f32[56,128]{1,0:T(8,128)}, u32[]{:S(2)}) copy-start(f32[56,128]{1,0:T(8,128)} %get-tuple-element.10) | copy-start | bytes 86020
  87.1 4.7 %collective-permute-start.3 = (bf16[64,56,128]{2,1,0:T(8,128)(2,1)S(1)}, bf16[64,56,128]{2,1,0:T(8,128)(2,1)S(1)}, u32[]{:S(2)}, u32[]{:S(2)}) collective-permute-start(bf16[64,56,128]{2,1,0:T(8,128)(2,1)S(1)} %all_to_all.10), channel_id=1, source_target_pairs={{0,8},{8,0},{1,9},{9,1},{2,10},{10,2},{3,11},{11,3},{4,12},{12,4},... | collective-permute-start | bytes 2752520 | tf_op jit(solution)/shard_map/ppermute | solution.py:19
  89.1 2.1 %collective-permute-start.2 = (f32[1,3584]{1,0:T(1,128)S(1)}, f32[1,3584]{1,0:T(1,128)S(1)}, u32[]{:S(2)}, u32[]{:S(2)}) collective-permute-start(f32[1,3584]{1,0:T(1,128)S(1)} %bitcast.22), channel_id=1, source_target_pairs={{0,8},{8,0},{1,9},{9,1},{2,10},{10,2},{3,11},{11,3},{4,12},{12,4},... | collective-permute-start | bytes 43016 | tf_op jit(solution)/shard_map/ppermute | solution.py:19

commit v2 on v0

v2 whole, which is shorter than its diff:
```python
import functools

import jax
import jax.numpy as jnp
from jax import lax
from jax.experimental import pallas as pl
from jax.experimental.pallas import tpu as pltpu
from jax.sharding import Mesh
from jax.sharding import PartitionSpec as P

AXIS = "d"
LANES = 128
CHIPS = 64


def device(i, core, s):
    return (i * 2 + core) * 8 + s


def place(d):
    return d // 16, d // 8 % 2, d % 8


def swap_pairs():
    pairs = []
    for d in range(128):
        i, core, s = place(d)
        pairs.append((d, device(i, 1 - core, s)))
    return pairs


def ring_pairs(step):
    pairs = []
    for d in range(128):
        i, core, s = place(d)
        if core == 0:
            pairs.append((d, device((i + 2 * step) % 8, core, s)))
        else:
            pairs.append((d, device(i, core, (s + 2 * step) % 8)))
    return pairs


def plane_groups():
    groups = [[device(2 * x + h, 0, s) for h in range(2) for s in range(8)] for x in range(4)]
    groups += [[device(i, 1, 2 * z + low) for low in range(2) for i in range(8)] for z in range(4)]
    return groups


def chip_groups():
    return [[device(i, core, s) for i in range(8) for s in range(8)] for core in range(2)]


def core_swap(x):
    return lax.ppermute(x, AXIS, swap_pairs())


def vmem(x):
    return pltpu.with_memory_space_constraint(x, pltpu.VMEM)


def hbm(x):
    return pltpu.with_memory_space_constraint(x, pltpu.HBM)


VMEM_SPEC = pl.BlockSpec(memory_space=pltpu.VMEM)
SMEM_SPEC = pl.BlockSpec(memory_space=pltpu.SMEM)
HBM_SPEC = pl.BlockSpec(memory_space=pltpu.HBM)
SCOPED = pltpu.CompilerParams(vmem_limit_bytes=8 * 2**20)


def my_core():
    return lax.axis_index(AXIS) // 8 % 2


def my_ring():
    d = lax.axis_index(AXIS)
    return jnp.where(d // 8 % 2 == 0, d // 32, d % 8 // 2)


def weigh_kernel(other, taking, counts, deltas, changes, out, held, arrived):
    core = my_core()
    owner = 1 - core if other else core
    chunks, pieces = held.shape[0], held.shape[3] // LANES
    block = 2 * pieces
    group = 8 * block + 8

    def fetch(source):
        for i in range(chunks):
            pltpu.make_async_copy(
                source.at[:, pl.ds(16 * i, 16), :], held.at[i], arrived.at[i]
            ).start()

    def fill(a0, a1, tail, by_chunk, by_row):
        for g in range(8):
            out[pl.ds(g * group + 8 * block, 8), :] = jnp.full((8, LANES), tail)

        def one(i, carry):
            pltpu.make_async_copy(
                deltas.at[:, pl.ds(0, 16), :], held.at[i], arrived.at[i]
            ).wait()
            for half in range(2):
                rows = pl.ds(half * 8, 8)
                for j in range(pieces):
                    lanes = pl.ds(j * LANES, LANES)
                    value = held[i, 0, rows, lanes].astype(jnp.float32) * a0
                    value = value + held[i, 1, rows, lanes].astype(jnp.float32) * a1
                    start = i * by_chunk + half * pieces + j
                    out[pl.ds(start, 8, stride=by_row), :] = value
            return carry

        lax.fori_loop(0, chunks, one, 0)

    t0, t1 = taking[0], taking[1]
    w0, w1 = t0 * counts[0], t1 * counts[1]

    @pl.when(owner == 0)
    def _():
        fetch(deltas)
        total = (w0 + w1).astype(jnp.float32)
        fill(w0.astype(jnp.float32), w1.astype(jnp.float32), total, group, block)

    @pl.when(owner == 1)
    def _():
        fetch(changes)
        fill(t0.astype(jnp.float32), t1.astype(jnp.float32), jnp.float32(0), block, group)


def weigh(other, taking, counts, deltas, changes):
    rows, columns = deltas.shape[1:]
    out_rows = 8 * (8 * 2 * columns // LANES + 8)
    return pl.pallas_call(
        functools.partial(weigh_kernel, other),
        in_specs=[SMEM_SPEC, SMEM_SPEC, HBM_SPEC, HBM_SPEC],
        out_specs=VMEM_SPEC,
        out_shape=pltpu.VMEM((out_rows, LANES), jnp.float32),
        scratch_shapes=[
            pltpu.VMEM((rows // 16, 2, 16, columns), deltas.dtype),
            pltpu.SemaphoreType.DMA((rows // 16,)),
        ],
        compiler_params=SCOPED,
        name="weigh_other" if other else "weigh_own",
    )(taking, counts, hbm(deltas), hbm(changes))


def join_kernel(keep, came, *outs):
    rows = outs[0].shape[0]
    mine = my_ring()
    for step, out in zip((2, 1, 3, 0), outs):
        at = pl.ds(pl.multiple_of((mine + step) % 4 * rows, 8), rows)
        out[...] = keep[at, :] + came[at, :]


def join(keep, came):
    out = pltpu.VMEM((keep.shape[0] // 4, LANES), jnp.float32)
    return pl.pallas_call(
        join_kernel,
        in_specs=[VMEM_SPEC, VMEM_SPEC],
        out_specs=[VMEM_SPEC] * 4,
        out_shape=[out] * 4,
        compiler_params=SCOPED,
        name="join",
    )(vmem(keep), vmem(came))


def fold_kernel(first, second, third, own, out):
    group = own.shape[0] // 2
    block = (group - 8) // 8

    def total(at, size):
        here = pl.ds(at, size)
        return own[here, :] + first[here, :] + second[here, :] + third[here, :]

    for g in range(2):
        tail = total(g * group + 8 * block, 8)
        for b in range(8):
            out[g * 8 + b, pl.ds(0, block), :] = total(g * group + b * block, block)
            out[g * 8 + b, pl.ds(block, 8), :] = tail


def fold(parts):
    group = parts[0].shape[0] // 2
    block = (group - 8) // 8
    return pl.pallas_call(
        fold_kernel,
        in_specs=[VMEM_SPEC] * 4,
        out_specs=VMEM_SPEC,
        out_shape=pltpu.VMEM((16, block + 8, LANES), jnp.float32),
        compiler_params=SCOPED,
        name="fold",
    )(*[vmem(p) for p in parts])


def update_kernel(client_count, blocks, params, variate, base, own, other, spread, total, fresh):
    core = my_core()
    count, used = blocks.shape[0], blocks.shape[1] - 8
    pieces = used // 2
    sums = blocks[0]
    for k in range(1, count):
        sums = sums + blocks[k]
    divisor = jnp.where(core == 0, sums[used : used + 1], jnp.float32(client_count))
    total[...] = sums[:used] / divisor
    for j in range(pieces):
        lanes = pl.ds(j * LANES, LANES)
        mine = jnp.where(core == 0, params[:, lanes], variate[:, lanes])
        mine = mine + total[pl.ds(core * pieces + j, 1), :]
        theirs = base[:, lanes] + total[pl.ds((1 - core) * pieces + j, 1), :]
        own[:, lanes] = mine
        other[:, lanes] = theirs
        fresh[pl.ds(core * pieces + j, 1), :] = mine
        fresh[pl.ds((1 - core) * pieces + j, 1), :] = theirs
    rounded = fresh[...].astype(jnp.bfloat16)
    for k in range(CHIPS):
        spread[k] = rounded


def update(blocks, params, variate, base, client_count):
    used = blocks.shape[1] - 8
    row = pltpu.VMEM(params.shape, jnp.float32)
    return pl.pallas_call(
        functools.partial(update_kernel, client_count),
        in_specs=[VMEM_SPEC] * 4,
        out_specs=[VMEM_SPEC] * 3,
        out_shape=[row, row, pltpu.VMEM((CHIPS, used, LANES), jnp.bfloat16)],
        scratch_shapes=[pltpu.VMEM((used, LANES), jnp.float32)] * 2,
        compiler_params=SCOPED,
        name="update",
    )(vmem(blocks), params, variate, vmem(base))


def to_rows(gathered):
    parts = gathered.reshape(8, 8, 2, -1)
    return jnp.transpose(parts, (0, 2, 1, 3)).reshape(128, -1)


def body(client_deltas, variate_deltas, params, variate, taking_part, counts):
    first = my_core() == 0
    client_count = 2 * 128

    send = weigh(True, taking_part, counts, client_deltas, variate_deltas)
    came = core_swap(send)
    keep = weigh(False, taking_part, counts, client_deltas, variate_deltas)
    base = core_swap(jnp.where(first, variate, params))

    *quarters, own_quarter = join(keep, came)
    arrived = [lax.ppermute(vmem(q), AXIS, ring_pairs(k)) for q, k in zip(quarters, (2, 1, 3))]
    plane = fold([*arrived, own_quarter])
    blocks = lax.all_to_all(vmem(plane), AXIS, 0, 0, axis_index_groups=plane_groups(), tiled=True)
    own_new, sent_new, spread = update(blocks, params, variate, base, client_count)

    other_new = core_swap(sent_new)
    new_params = jnp.where(first, own_new, other_new)
    new_variate = jnp.where(first, other_new, own_new)

    gathered = lax.all_to_all(spread, AXIS, 0, 0, axis_index_groups=chip_groups(), tiled=True)
    own_rows = to_rows(gathered)
    other_rows = to_rows(core_swap(gathered))
    client_params = jnp.where(first, own_rows, other_rows)
    client_variate = jnp.where(first, other_rows, own_rows)
    return (new_params, new_variate, client_params, client_variate)


def solution(mesh):
    flat = Mesh(mesh.devices.reshape(-1), (AXIS,))
    split = P(AXIS)
    in_specs = (split, split, split, split, split, split)
    out_specs = (split, split, P(), P())
    return jax.shard_map(body, mesh=flat, in_specs=in_specs, out_specs=out_specs, check_vma=False)
```

time: 516 us -> 72.1 us (0.14)
  waiting for transfers between devices: 388 us -> 20.1 us
  blocking collectives: 69 us -> 20 us
  other arithmetic: 22.9 us -> 0.77 us
  starting transfers between devices: 0.08 us -> 20.7 us
  between operations: 14.8 us -> 0.73 us
  local copies, waits for them, and re-layouts: 14.6 us -> 3.8 us
  Pallas kernels: 0 us -> 5.69 us
  matrix products: 5.62 us -> 0 us
    all_gather x1 -> x0, waiting for transfers between devices: 303 us -> none  [in_one_piece(): result = lax.all_gather(both, axis, axis=dim, tiled=True)]
    unnamed x3 -> x0, waiting for transfers between devices: 85.7 us -> none
    unnamed x1 -> x0, blocking collectives: 69 us -> none
    all_to_all x0 -> x1, blocking collectives: none -> 20 us  [body(): lax.all_to_all(spread, AXIS, 0, 0, axis_index_groups=chip_groups(), tiled...]
    add x1 -> x0, other arithmetic: 16.5 us -> none  [weigh_blocks(): moved_sum[0] + moved_sum[1]]
    ppermute x0 -> x7, starting transfers between devices: none -> 13.9 us  [the longest x4 7.45 us: core_swap(): return lax.ppermute(x, AXIS, swap_pairs())]
    ppermute x0 -> x7, waiting for transfers between devices: none -> 13.2 us  [the longest x3 9.06 us: body(): lax.ppermute(vmem(q), AXIS, ring_pairs(k))]
    all_to_all x0 -> x1, waiting for transfers between devices: none -> 6.85 us  [body(): lax.all_to_all(vmem(plane), AXIS, 0, 0, axis_index_groups=plane_groups(),...]
  transfers between devices with their start and end apart: 2 -> 8, of which waited for: 2 -> 7; matrix products, arithmetic and copies ran while one was open for 0% -> 1% of each run, Pallas kernels for 0% -> 3%
where the time goes in v2:
time: 72.1 us; the launch traced here: 71.8 us
  starting transfers between devices  20.7 us (29%)
  waiting for transfers between devices  20.1 us (28%)
  blocking collectives  20 us (28%)
  Pallas kernels  5.69 us (8%)
  local copies, waits for them, and re-layouts  3.8 us (5%)
  other arithmetic  0.77 us (1%)
  between operations  0.73 us (1%)
    all_to_all x1, blocking collectives, body(): lax.all_to_all(spread, AXIS, 0, 0, axis_index_groups=chip_groups(), tiled...  20 us
    ppermute x3, waiting for transfers between devices, body(): lax.ppermute(vmem(q), AXIS, ring_pairs(k))  9.06 us
    ppermute x4, starting transfers between devices, core_swap(): return lax.ppermute(x, AXIS, swap_pairs())  7.45 us
    all_to_all x1, waiting for transfers between devices, body(): lax.all_to_all(vmem(plane), AXIS, 0, 0, axis_index_groups=plane_groups(),...  6.85 us
    all_to_all x1, starting transfers between devices, body(): lax.all_to_all(vmem(plane), AXIS, 0, 0, axis_index_groups=plane_groups(),...  6.75 us
    ppermute x3, starting transfers between devices, body(): lax.ppermute(vmem(q), AXIS, ring_pairs(k))  6.46 us
    pallas_call x2, Pallas kernels, weigh(): pl.pallas_call(functools.partial(weigh_kernel, other), in_specs=[SMEM_SPE...  4.46 us
    ppermute x4, waiting for transfers between devices, core_swap(): return lax.ppermute(x, AXIS, swap_pairs())  4.17 us
  transfers between devices with their start and end apart: 8, of which 7 were waited for; matrix products, arithmetic and copies ran while one was open for 1% of the time, Pallas kernels for 3%

profile of v2, /device:TPU:1, one launch (start us, length us, event | category | flops | bytes accessed | tf_op | source)
XLA Modules:
  0.0 71.8 jit_solution(2170456865021492744)
XLA Ops:
  0.6 0.0 copy-start.2
  0.6 0.6 copy-done.2
  1.3 0.0 copy-start.3
  1.3 0.7 copy-done.3
  1.9 2.2 %weigh_other.1 = f32[3648,128]{1,0:T(8,128)S(1)} custom-call(s32[2]{0:T(128)S(1)} %copy-done.2, s32[2]{0:T(128)S(1)} %copy-done.3, bf16[2,128,3584]{2,1,0:T(8,128)(2,1)} %deltas.3, bf16[2,128,3584]{2,1,0:T(8,128)(2,1)} %changes.3), custom_call_target="tpu_custom_call" | custom-call | tf_op jit(solution)/shard_map/weigh_other/pallas_call | solution.py:131
  4.2 1.5 %collective-permute-start = (f32[3648,128]{1,0:T(8,128)S(1)}, f32[3648,128]{1,0:T(8,128)S(1)}, u32[]{:S(2)}, u32[]{:S(2)}) collective-permute-start(f32[3648,128]{1,0:T(8,128)S(1)} %weigh_other.1), channel_id=1, source_target_pairs={{0,8},{1,9},{2,10},{3,11},{4,12},{5,13},{6,14},{7,15},{8,0},{9,1},... | collective-permute-start | bytes 5603336 | tf_op jit(solution)/shard_map/ppermute | solution.py:54
  5.6 2.2 %weigh_own.1.keep = f32[3648,128]{1,0:T(8,128)S(1)} custom-call(s32[2]{0:T(128)S(1)} %copy-done.2, s32[2]{0:T(128)S(1)} %copy-done.3, bf16[2,128,3584]{2,1,0:T(8,128)(2,1)} %deltas.3, bf16[2,128,3584]{2,1,0:T(8,128)(2,1)} %changes.3), custom_call_target="tpu_custom_call" | custom-call | tf_op jit(solution)/shard_map/weigh_own/pallas_call | solution.py:131
  7.9 1.2 %collective-permute-done.came = f32[3648,128]{1,0:T(8,128)S(1)} collective-permute-done((f32[3648,128]{1,0:T(8,128)S(1)}, f32[3648,128]{1,0:T(8,128)S(1)}, u32[]{:S(2)}, u32[]{:S(2)}) %collective-permute-start) | collective-permute-done | bytes 1867808 | tf_op jit(solution)/shard_map/ppermute | solution.py:54
  9.1 0.2 join.1
  9.3 0.0 copy-start
  9.3 0.0 copy-start.1
  9.3 3.8 %collective-permute-start.1 = (f32[912,128]{1,0:T(8,128)S(1)}, f32[912,128]{1,0:T(8,128)S(1)}, u32[]{:S(2)}, u32[]{:S(2)}) collective-permute-start(f32[912,128]{1,0:T(8,128)S(1)} %get-tuple-element.11), channel_id=1, source_target_pairs={{0,64},{1,65},{2,66},{3,67},{4,68},{5,69},{6,70},{7,71},{8,12},{9,... | collective-permute-start | bytes 1400840 | tf_op jit(solution)/shard_map/ppermute | solution.py:245
  13.1 0.7 %collective-permute-start.2 = (f32[912,128]{1,0:T(8,128)S(1)}, f32[912,128]{1,0:T(8,128)S(1)}, u32[]{:S(2)}, u32[]{:S(2)}) collective-permute-start(f32[912,128]{1,0:T(8,128)S(1)} %get-tuple-element.12), channel_id=1, source_target_pairs={{0,32},{1,33},{2,34},{3,35},{4,36},{5,37},{6,38},{7,39},{8,10},{9,... | collective-permute-start | bytes 1400840 | tf_op jit(solution)/shard_map/ppermute | solution.py:245
  13.8 1.9 %collective-permute-start.3 = (f32[912,128]{1,0:T(8,128)S(1)}, f32[912,128]{1,0:T(8,128)S(1)}, u32[]{:S(2)}, u32[]{:S(2)}) collective-permute-start(f32[912,128]{1,0:T(8,128)S(1)} %get-tuple-element.13), channel_id=1, source_target_pairs={{0,96},{1,97},{2,98},{3,99},{4,100},{5,101},{6,102},{7,103},{8,14}... | collective-permute-start | bytes 1400840 | tf_op jit(solution)/shard_map/ppermute | solution.py:245
  15.8 3.6 %collective-permute-done.1.first = f32[912,128]{1,0:T(8,128)S(1)} collective-permute-done((f32[912,128]{1,0:T(8,128)S(1)}, f32[912,128]{1,0:T(8,128)S(1)}, u32[]{:S(2)}, u32[]{:S(2)}) %collective-permute-start.1) | collective-permute-done | bytes 466976 | tf_op jit(solution)/shard_map/ppermute | solution.py:245
  19.4 5.0 %collective-permute-done.2.second = f32[912,128]{1,0:T(8,128)S(1)} collective-permute-done((f32[912,128]{1,0:T(8,128)S(1)}, f32[912,128]{1,0:T(8,128)S(1)}, u32[]{:S(2)}, u32[]{:S(2)}) %collective-permute-start.2) | collective-permute-done | bytes 466976 | tf_op jit(solution)/shard_map/ppermute | solution.py:245
  24.4 0.5 collective-permute-done.3.third
  24.8 0.9 %fold.1 = f32[16,64,128]{2,1,0:T(8,128)} custom-call(f32[912,128]{1,0:T(8,128)S(1)} %collective-permute-done.1.first, f32[912,128]{1,0:T(8,128)S(1)} %collective-permute-done.2.second, f32[912,128]{1,0:T(8,128)S(1)} %collective-permute-done.3.third, f32[912,128]{1,0:T(8,128)S(1)} %get-tuple-element.14.own), custom_call_target="tpu_custom_call" | custom-call | tf_op jit(solution)/shard_map/fold/pallas_call | solution.py:183
  25.8 6.8 %all-to-all-start = ((f32[16,64,128]{2,1,0:T(8,128)}), f32[16,64,128]{2,1,0:T(8,128)S(1)}, u32[]{:S(2)}, u32[]{:S(2)}) async-start(f32[16,64,128]{2,1,0:T(8,128)} %fold.1), calls=%async_computation | async-start | bytes 1048576 | tf_op jit(solution)/shard_map/all_to_all | solution.py:247
  32.5 0.0 copy-done
  32.5 0.0 copy-done.1
  32.6 1.6 %collective-permute-start.4 = (f32[1,3584]{1,0:T(1,128)S(1)}, f32[1,3584]{1,0:T(1,128)S(1)}, u32[]{:S(2)}, u32[]{:S(2)}) collective-permute-start(f32[1,3584]{1,0:T(1,128)S(1)} %broadcast_select_fusion.4), channel_id=1, source_target_pairs={{0,8},{1,9},{2,10},{3,11},{4,12},{5,13},{6,14},{7,15},{8,0},{9,1},... | collective-permute-start | bytes 43016 | tf_op jit(solution)/shard_map/ppermute | solution.py:54
  34.2 0.8 %collective-permute-done.4.base = f32[1,3584]{1,0:T(1,128)S(1)} collective-permute-done((f32[1,3584]{1,0:T(1,128)S(1)}, f32[1,3584]{1,0:T(1,128)S(1)}, u32[]{:S(2)}, u32[]{:S(2)}) %collective-permute-start.4) | collective-permute-done | bytes 14368 | tf_op jit(solution)/shard_map/ppermute | solution.py:54
  35.0 6.8 %all-to-all-done.blocks = f32[16,64,128]{2,1,0:T(8,128)S(1)} async-done(((f32[16,64,128]{2,1,0:T(8,128)}), f32[16,64,128]{2,1,0:T(8,128)S(1)}, u32[]{:S(2)}, u32[]{:S(2)}) %all-to-all-start) | async-done | bytes 524320 | tf_op jit(solution)/shard_map/all_to_all | solution.py:247
  41.9 0.1 update.1
  42.0 20.0 %all_to_all.10 = bf16[64,56,128]{2,1,0:T(8,128)(2,1)S(1)} all-to-all(bf16[64,56,128]{2,1,0:T(8,128)(2,1)S(1)} %get-tuple-element.17), channel_id=1, replica_groups={{0,1,2,3,4,5,6,7,16,17,18,19,20,21,22,23,32,33,34,35,36,37,38,39,48,49,..., dimensions={0} | all-to-all | bytes 1835008 | tf_op jit(solution)/shard_map/all_to_all | solution.py:254
  62.0 4.4 %collective-permute-start.6 = (bf16[64,56,128]{2,1,0:T(8,128)(2,1)S(1)}, bf16[64,56,128]{2,1,0:T(8,128)(2,1)S(1)}, u32[]{:S(2)}, u32[]{:S(2)}) collective-permute-start(bf16[64,56,128]{2,1,0:T(8,128)(2,1)S(1)} %all_to_all.10), channel_id=1, source_target_pairs={{0,8},{1,9},{2,10},{3,11},{4,12},{5,13},{6,14},{7,15},{8,0},{9,1},... | collective-permute-start | bytes 2752520 | tf_op jit(solution)/shard_map/ppermute | solution.py:54
  66.4 0.0 collective-permute-start.5
  66.4 2.1 %collective-permute-done.5 = f32[1,3584]{1,0:T(1,128)S(1)} collective-permute-done((f32[1,3584]{1,0:T(1,128)S(1)}, f32[1,3584]{1,0:T(1,128)S(1)}, u32[]{:S(2)}, u32[]{:S(2)}) %collective-permute-start.5) | collective-permute-done | bytes 14368 | tf_op jit(solution)/shard_map/ppermute | solution.py:54
  68.5 0.6 broadcast_select_fusion.2
  69.2 0.0 collective-permute-done.6
  69.2 0.1 broadcast_select_fusion
  69.3 0.2 select_n.67
  69.5 1.0 %copy.10 = bf16[8,2,8,3584]{3,2,1,0:T(8,128)(2,1)} copy(bf16[8,2,8,3584]{3,1,2,0:T(2,128)(2,1)S(1)} %bitcast.4) | data formatting | bytes 1835008 | tf_op jit(solution)/shard_map/jit(_where)/select_n | solution.py:257
  70.5 0.2 select_n.71
  70.8 1.0 %copy.11 = bf16[8,2,8,3584]{3,2,1,0:T(8,128)(2,1)} copy(bf16[8,2,8,3584]{3,1,2,0:T(2,128)(2,1)S(1)} %bitcast.5) | data formatting | bytes 1835008 | tf_op jit(solution)/shard_map/jit(_where)/select_n | solution.py:258
  (1 shorter events, 0.0 us)
Async XLA Ops:
  0.6 0.7 copy-start.2
  1.3 0.7 copy-start.3
  4.2 4.9 %collective-permute-start = (f32[3648,128]{1,0:T(8,128)S(1)}, f32[3648,128]{1,0:T(8,128)S(1)}, u32[]{:S(2)}, u32[]{:S(2)}) collective-permute-start(f32[3648,128]{1,0:T(8,128)S(1)} %weigh_other.1), channel_id=1, source_target_pairs={{0,8},{1,9},{2,10},{3,11},{4,12},{5,13},{6,14},{7,15},{8,0},{9,1},... | collective-permute-start | bytes 5603336 | tf_op jit(solution)/shard_map/ppermute | solution.py:54
  9.3 23.2 %copy-start = (f32[1,3584]{1,0:T(1,128)S(1)}, f32[1,3584]{1,0:T(1,128)}, u32[]{:S(2)}) copy-start(f32[1,3584]{1,0:T(1,128)} %params.1) | copy-start | bytes 43012
  9.3 23.2 %copy-start.1 = (f32[1,3584]{1,0:T(1,128)S(1)}, f32[1,3584]{1,0:T(1,128)}, u32[]{:S(2)}) copy-start(f32[1,3584]{1,0:T(1,128)} %variate.1) | copy-start | bytes 43012
  9.3 10.1 %collective-permute-start.1 = (f32[912,128]{1,0:T(8,128)S(1)}, f32[912,128]{1,0:T(8,128)S(1)}, u32[]{:S(2)}, u32[]{:S(2)}) collective-permute-start(f32[912,128]{1,0:T(8,128)S(1)} %get-tuple-element.11), channel_id=1, source_target_pairs={{0,64},{1,65},{2,66},{3,67},{4,68},{5,69},{6,70},{7,71},{8,12},{9,... | collective-permute-start | bytes 1400840 | tf_op jit(solution)/shard_map/ppermute | solution.py:245
  13.1 11.3 %collective-permute-start.2 = (f32[912,128]{1,0:T(8,128)S(1)}, f32[912,128]{1,0:T(8,128)S(1)}, u32[]{:S(2)}, u32[]{:S(2)}) collective-permute-start(f32[912,128]{1,0:T(8,128)S(1)} %get-tuple-element.12), channel_id=1, source_target_pairs={{0,32},{1,33},{2,34},{3,35},{4,36},{5,37},{6,38},{7,39},{8,10},{9,... | collective-permute-start | bytes 1400840 | tf_op jit(solution)/shard_map/ppermute | solution.py:245
  13.8 11.0 %collective-permute-start.3 = (f32[912,128]{1,0:T(8,128)S(1)}, f32[912,128]{1,0:T(8,128)S(1)}, u32[]{:S(2)}, u32[]{:S(2)}) collective-permute-start(f32[912,128]{1,0:T(8,128)S(1)} %get-tuple-element.13), channel_id=1, source_target_pairs={{0,96},{1,97},{2,98},{3,99},{4,100},{5,101},{6,102},{7,103},{8,14}... | collective-permute-start | bytes 1400840 | tf_op jit(solution)/shard_map/ppermute | solution.py:245
  25.8 16.1 %all-to-all-start = ((f32[16,64,128]{2,1,0:T(8,128)}), f32[16,64,128]{2,1,0:T(8,128)S(1)}, u32[]{:S(2)}, u32[]{:S(2)}) async-start(f32[16,64,128]{2,1,0:T(8,128)} %fold.1), calls=%async_computation | async-start | bytes 1048576 | tf_op jit(solution)/shard_map/all_to_all | solution.py:247
  32.6 2.4 %collective-permute-start.4 = (f32[1,3584]{1,0:T(1,128)S(1)}, f32[1,3584]{1,0:T(1,128)S(1)}, u32[]{:S(2)}, u32[]{:S(2)}) collective-permute-start(f32[1,3584]{1,0:T(1,128)S(1)} %broadcast_select_fusion.4), channel_id=1, source_target_pairs={{0,8},{1,9},{2,10},{3,11},{4,12},{5,13},{6,14},{7,15},{8,0},{9,1},... | collective-permute-start | bytes 43016 | tf_op jit(solution)/shard_map/ppermute | solution.py:54
  62.0 7.1 %collective-permute-start.6 = (bf16[64,56,128]{2,1,0:T(8,128)(2,1)S(1)}, bf16[64,56,128]{2,1,0:T(8,128)(2,1)S(1)}, u32[]{:S(2)}, u32[]{:S(2)}) collective-permute-start(bf16[64,56,128]{2,1,0:T(8,128)(2,1)S(1)} %all_to_all.10), channel_id=1, source_target_pairs={{0,8},{1,9},{2,10},{3,11},{4,12},{5,13},{6,14},{7,15},{8,0},{9,1},... | collective-permute-start | bytes 2752520 | tf_op jit(solution)/shard_map/ppermute | solution.py:54
  66.4 2.1 %collective-permute-start.5 = (f32[1,3584]{1,0:T(1,128)S(1)}, f32[1,3584]{1,0:T(1,128)S(1)}, u32[]{:S(2)}, u32[]{:S(2)}) collective-permute-start(f32[1,3584]{1,0:T(1,128)S(1)} %get-tuple-element.16), channel_id=1, source_target_pairs={{0,8},{1,9},{2,10},{3,11},{4,12},{5,13},{6,14},{7,15},{8,0},{9,1},... | collective-permute-start | bytes 43016 | tf_op jit(solution)/shard_map/ppermute | solution.py:54

commit v3 on v2

--- a/solution.py
+++ b/solution.py
@@ -63,7 +63,6 @@
 
 
 VMEM_SPEC = pl.BlockSpec(memory_space=pltpu.VMEM)
-SMEM_SPEC = pl.BlockSpec(memory_space=pltpu.SMEM)
 HBM_SPEC = pl.BlockSpec(memory_space=pltpu.HBM)
 SCOPED = pltpu.CompilerParams(vmem_limit_bytes=8 * 2**20)
 
@@ -77,7 +76,9 @@
     return jnp.where(d // 8 % 2 == 0, d // 32, d % 8 // 2)
 
 
-def weigh_kernel(other, taking, counts, deltas, changes, out, held, arrived):
+def weigh_kernel(
+    other, taking_hbm, counts_hbm, deltas, changes, out, held, taking, counts, arrived, small
+):
     core = my_core()
     owner = 1 - core if other else core
     chunks, pieces = held.shape[0], held.shape[3] // LANES
@@ -110,18 +111,33 @@
 
         lax.fori_loop(0, chunks, one, 0)
 
+    scalars = [
+        pltpu.make_async_copy(taking_hbm, taking, small.at[0]),
+        pltpu.make_async_copy(counts_hbm, counts, small.at[1]),
+    ]
+    for copy in scalars:
+        copy.start()
+
+    @pl.when(owner == 0)
+    def _():
+        fetch(deltas)
+
+    @pl.when(owner == 1)
+    def _():
+        fetch(changes)
+
+    for copy in scalars:
+        copy.wait()
     t0, t1 = taking[0], taking[1]
     w0, w1 = t0 * counts[0], t1 * counts[1]
 
     @pl.when(owner == 0)
     def _():
-        fetch(deltas)
         total = (w0 + w1).astype(jnp.float32)
         fill(w0.astype(jnp.float32), w1.astype(jnp.float32), total, group, block)
 
     @pl.when(owner == 1)
     def _():
-        fetch(changes)
         fill(t0.astype(jnp.float32), t1.astype(jnp.float32), jnp.float32(0), block, group)
 
 
@@ -130,22 +146,25 @@
     out_rows = 8 * (8 * 2 * columns // LANES + 8)
     return pl.pallas_call(
         functools.partial(weigh_kernel, other),
-        in_specs=[SMEM_SPEC, SMEM_SPEC, HBM_SPEC, HBM_SPEC],
+        in_specs=[HBM_SPEC] * 4,
         out_specs=VMEM_SPEC,
         out_shape=pltpu.VMEM((out_rows, LANES), jnp.float32),
         scratch_shapes=[
             pltpu.VMEM((rows // 16, 2, 16, columns), deltas.dtype),
+            pltpu.SMEM(taking.shape, jnp.int32),
+            pltpu.SMEM(counts.shape, jnp.int32),
             pltpu.SemaphoreType.DMA((rows // 16,)),
+            pltpu.SemaphoreType.DMA((2,)),
         ],
         compiler_params=SCOPED,
         name="weigh_other" if other else "weigh_own",
-    )(taking, counts, hbm(deltas), hbm(changes))
+    )(hbm(taking), hbm(counts), hbm(deltas), hbm(changes))
 
 
 def join_kernel(keep, came, *outs):
     rows = outs[0].shape[0]
     mine = my_ring()
-    for step, out in zip((2, 1, 3, 0), outs):
+    for step, out in zip((1, 3, 2, 0), outs):
         at = pl.ds(pl.multiple_of((mine + step) % 4 * rows, 8), rows)
         out[...] = keep[at, :] + came[at, :]
 
@@ -227,9 +246,99 @@
     )(vmem(blocks), params, variate, vmem(base))
 
 
-def to_rows(gathered):
-    parts = gathered.reshape(8, 8, 2, -1)
-    return jnp.transpose(parts, (0, 2, 1, 3)).reshape(128, -1)
+def lay_out(source, wide, put, done=lambda i: None):
+    chips, block = source.shape[:2]
+    pieces = block // 2
+    for k in range(chips):
+        wide[pl.ds(k * block, block), :] = source[k].astype(jnp.float32)
+
+    def one(i, carry):
+        for j in range(pieces):
+            rows = [wide[pl.ds(i * 8 * block + c * pieces + j, 8, stride=block), :] for c in (0, 1)]
+            put(i, j, jnp.concatenate(rows).astype(jnp.bfloat16))
+        done(i)
+        return carry
+
+    lax.fori_loop(0, 8, one, 0)
+
+
+def lay_kernel(source, out, wide):
+    def put(i, j, value):
+        at = pl.ds(pl.multiple_of(i * 16, 16), 16)
+        out[at, pl.ds(j * LANES, LANES)] = value
+
+    lay_out(source, wide, put)
+
+
+def lay(gathered):
+    chips, block = gathered.shape[:2]
+    return pl.pallas_call(
+        lay_kernel,
+        in_specs=[VMEM_SPEC],
+        out_specs=VMEM_SPEC,
+        out_shape=pltpu.VMEM((2 * chips, block // 2 * LANES), jnp.bfloat16),
+        scratch_shapes=[pltpu.VMEM((chips * block, LANES), jnp.float32)],
+        compiler_params=SCOPED,
+        name="lay",
+    )(vmem(gathered))
+
+
+def finish_kernel(own_rows, swapped, own_new, other_new, *refs):
+    outs, wide, laid, sems = refs[:4], refs[4], refs[5], refs[6]
+    core = my_core()
+
+    def place_all(mine, theirs, mine_rows, their_rows):
+        copies = [
+            pltpu.make_async_copy(own_new, mine, sems.at[0]),
+            pltpu.make_async_copy(other_new, theirs, sems.at[1]),
+            pltpu.make_async_copy(own_rows, mine_rows, sems.at[2]),
+        ]
+        for copy in copies:
+            copy.start()
+
+        def put(i, j, value):
+            at = pl.ds(pl.multiple_of(i * 16, 16), 16)
+            laid[at, pl.ds(j * LANES, LANES)] = value
+
+        def write(i):
+            at = pl.ds(pl.multiple_of(i * 16, 16), 16)
+            return pltpu.make_async_copy(laid.at[at, :], their_rows.at[at, :], sems.at[3 + i])
+
+        lay_out(swapped, wide, put, lambda i: write(i).start())
+        for copy in copies:
+            copy.wait()
+        for i in range(8):
+            write(i).wait()
+
+    @pl.when(core == 0)
+    def _():
+        place_all(outs[0], outs[1], outs[2], outs[3])
+
+    @pl.when(core == 1)
+    def _():
+        place_all(outs[1], outs[0], outs[3], outs[2])
+
+
+def finish(own_rows, swapped, own_new, other_new):
+    chips, block = swapped.shape[:2]
+    return pl.pallas_call(
+        finish_kernel,
+        in_specs=[VMEM_SPEC] * 4,
+        out_specs=[HBM_SPEC] * 4,
+        out_shape=[
+            jax.ShapeDtypeStruct(own_new.shape, jnp.float32),
+            jax.ShapeDtypeStruct(own_new.shape, jnp.float32),
+            jax.ShapeDtypeStruct(own_rows.shape, jnp.bfloat16),
+            jax.ShapeDtypeStruct(own_rows.shape, jnp.bfloat16),
+        ],
+        scratch_shapes=[
+            pltpu.VMEM((chips * block, LANES), jnp.float32),
+            pltpu.VMEM(own_rows.shape, jnp.bfloat16),
+            pltpu.SemaphoreType.DMA((11,)),
+        ],
+        compiler_params=SCOPED,
+        name="finish",
+    )(vmem(own_rows), vmem(swapped), vmem(own_new), vmem(other_new))
 
 
 def body(client_deltas, variate_deltas, params, variate, taking_part, counts):
@@ -242,21 +351,16 @@
     base = core_swap(jnp.where(first, variate, params))
 
     *quarters, own_quarter = join(keep, came)
-    arrived = [lax.ppermute(vmem(q), AXIS, ring_pairs(k)) for q, k in zip(quarters, (2, 1, 3))]
+    arrived = [lax.ppermute(vmem(q), AXIS, ring_pairs(k)) for q, k in zip(quarters, (1, 3, 2))]
     plane = fold([*arrived, own_quarter])
     blocks = lax.all_to_all(vmem(plane), AXIS, 0, 0, axis_index_groups=plane_groups(), tiled=True)
     own_new, sent_new, spread = update(blocks, params, variate, base, client_count)
 
     other_new = core_swap(sent_new)
-    new_params = jnp.where(first, own_new, other_new)
-    new_variate = jnp.where(first, other_new, own_new)
-
     gathered = lax.all_to_all(spread, AXIS, 0, 0, axis_index_groups=chip_groups(), tiled=True)
-    own_rows = to_rows(gathered)
-    other_rows = to_rows(core_swap(gathered))
-    client_params = jnp.where(first, own_rows, other_rows)
-    client_variate = jnp.where(first, other_rows, own_rows)
-    return (new_params, new_variate, client_params, client_variate)
+    swapped = core_swap(gathered)
+    own_rows = lay(gathered)
+    return tuple(finish(own_rows, swapped, own_new, other_new))
 
 
 def solution(mesh):

time: 72.1 us -> 68 us (0.943)
  local copies, waits for them, and re-layouts: 3.8 us -> 0.01 us
  waiting for transfers between devices: 20.1 us -> 21.9 us
  blocking collectives: 20 us -> 18.9 us
  starting transfers between devices: 20.7 us -> 19.8 us
  Pallas kernels: 5.69 us -> 6.44 us
  other arithmetic: 0.77 us -> 0.02 us
    select_n x4 -> x0, local copies, waits for them, and re-layouts: 2.48 us -> none  [the longest x2 1.24 us: body(): client_params = jnp.where(first, own_rows, other_rows)]
    ppermute x3, waiting for transfers between devices: 9.06 us -> 10.8 us  [body(): lax.ppermute(vmem(q), AXIS, ring_pairs(k))]
    unnamed x8 -> x4, local copies, waits for them, and re-layouts: 1.32 us -> 0.01 us
    ppermute x3, starting transfers between devices: 6.46 us -> 5.24 us  [body(): lax.ppermute(vmem(q), AXIS, ring_pairs(k))]
    all_to_all x1, blocking collectives: 20 us -> 18.9 us  [body(): lax.all_to_all(spread, AXIS, 0, 0, axis_index_groups=chip_groups(), tiled...]
    select_n x2 -> x0, other arithmetic: 0.75 us -> none  [the longest x1 0.63 us: body(): new_variate = jnp.where(first, other_new, own_new)]
    pallas_call x2 -> x4, Pallas kernels: 4.46 us -> 5.2 us  [the longest x2 3.38 us: weigh(): pl.pallas_call(functools.partial(weigh_kernel, other), in_specs=[HBM_SPEC...]
  transfers between devices with their start and end apart: 8 -> 8, of which waited for: 7 -> 7; matrix products, arithmetic and copies ran while one was open for 1% -> 0% of each run, Pallas kernels for 3% -> 3%
where the time goes in v3:
time: 68 us; the launch traced here: 67.7 us
  waiting for transfers between devices  21.9 us (32%)
  starting transfers between devices  19.8 us (29%)
  blocking collectives  18.9 us (28%)
  Pallas kernels  6.44 us (9%)
  between operations  0.72 us (1%)
    all_to_all x1, blocking collectives, body(): lax.all_to_all(spread, AXIS, 0, 0, axis_index_groups=chip_groups(), tiled...  18.9 us
    ppermute x3, waiting for transfers between devices, body(): lax.ppermute(vmem(q), AXIS, ring_pairs(k))  10.8 us
    ppermute x4, starting transfers between devices, core_swap(): return lax.ppermute(x, AXIS, swap_pairs())  7.75 us
    all_to_all x1, waiting for transfers between devices, body(): lax.all_to_all(vmem(plane), AXIS, 0, 0, axis_index_groups=plane_groups(),...  6.84 us
    all_to_all x1, starting transfers between devices, body(): lax.all_to_all(vmem(plane), AXIS, 0, 0, axis_index_groups=plane_groups(),...  6.75 us
    ppermute x3, starting transfers between devices, body(): lax.ppermute(vmem(q), AXIS, ring_pairs(k))  5.24 us
    ppermute x4, waiting for transfers between devices, core_swap(): return lax.ppermute(x, AXIS, swap_pairs())  4.21 us
    pallas_call x2, Pallas kernels, weigh(): pl.pallas_call(functools.partial(weigh_kernel, other), in_specs=[HBM_SPEC...  3.38 us
  transfers between devices with their start and end apart: 8, of which 7 were waited for; matrix products, arithmetic and copies ran while one was open for 0% of the time, Pallas kernels for 3%

profile of v3, /device:TPU:1, one launch (start us, length us, event | category | flops | bytes accessed | tf_op | source)
XLA Modules:
  0.0 67.7 jit_solution(2803575176653792348)
XLA Ops:
  0.6 1.7 %weigh_other.1 = f32[3648,128]{1,0:T(8,128)S(1)} custom-call(s32[2]{0:T(128)} %taking_hbm.3, s32[2]{0:T(128)} %counts_hbm.3, bf16[2,128,3584]{2,1,0:T(8,128)(2,1)} %deltas.3, bf16[2,128,3584]{2,1,0:T(8,128)(2,1)} %changes.3), custom_call_target="tpu_custom_call" | custom-call | tf_op jit(solution)/shard_map/weigh_other/pallas_call | solution.py:147
  2.3 1.5 %collective-permute-start = (f32[3648,128]{1,0:T(8,128)S(1)}, f32[3648,128]{1,0:T(8,128)S(1)}, u32[]{:S(2)}, u32[]{:S(2)}) collective-permute-start(f32[3648,128]{1,0:T(8,128)S(1)} %weigh_other.1), channel_id=1, source_target_pairs={{0,8},{1,9},{2,10},{3,11},{4,12},{5,13},{6,14},{7,15},{8,0},{9,1},... | collective-permute-start | bytes 5603336 | tf_op jit(solution)/shard_map/ppermute | solution.py:54
  3.8 1.7 %weigh_own.1.keep = f32[3648,128]{1,0:T(8,128)S(1)} custom-call(s32[2]{0:T(128)} %taking_hbm.3, s32[2]{0:T(128)} %counts_hbm.3, bf16[2,128,3584]{2,1,0:T(8,128)(2,1)} %deltas.3, bf16[2,128,3584]{2,1,0:T(8,128)(2,1)} %changes.3), custom_call_target="tpu_custom_call" | custom-call | tf_op jit(solution)/shard_map/weigh_own/pallas_call | solution.py:147
  5.5 1.8 %collective-permute-done.came = f32[3648,128]{1,0:T(8,128)S(1)} collective-permute-done((f32[3648,128]{1,0:T(8,128)S(1)}, f32[3648,128]{1,0:T(8,128)S(1)}, u32[]{:S(2)}, u32[]{:S(2)}) %collective-permute-start) | collective-permute-done | bytes 1867808 | tf_op jit(solution)/shard_map/ppermute | solution.py:54
  7.3 0.2 join.1
  7.5 0.0 copy-start
  7.5 0.0 copy-start.1
  7.5 1.8 %collective-permute-start.1 = (f32[912,128]{1,0:T(8,128)S(1)}, f32[912,128]{1,0:T(8,128)S(1)}, u32[]{:S(2)}, u32[]{:S(2)}) collective-permute-start(f32[912,128]{1,0:T(8,128)S(1)} %get-tuple-element.11), channel_id=1, source_target_pairs={{0,32},{1,33},{2,34},{3,35},{4,36},{5,37},{6,38},{7,39},{8,10},{9,... | collective-permute-start | bytes 1400840 | tf_op jit(solution)/shard_map/ppermute | solution.py:354
  9.3 2.2 %collective-permute-start.2 = (f32[912,128]{1,0:T(8,128)S(1)}, f32[912,128]{1,0:T(8,128)S(1)}, u32[]{:S(2)}, u32[]{:S(2)}) collective-permute-start(f32[912,128]{1,0:T(8,128)S(1)} %get-tuple-element.12), channel_id=1, source_target_pairs={{0,96},{1,97},{2,98},{3,99},{4,100},{5,101},{6,102},{7,103},{8,14}... | collective-permute-start | bytes 1400840 | tf_op jit(solution)/shard_map/ppermute | solution.py:354
  11.5 1.2 %collective-permute-start.3 = (f32[912,128]{1,0:T(8,128)S(1)}, f32[912,128]{1,0:T(8,128)S(1)}, u32[]{:S(2)}, u32[]{:S(2)}) collective-permute-start(f32[912,128]{1,0:T(8,128)S(1)} %get-tuple-element.13), channel_id=1, source_target_pairs={{0,64},{1,65},{2,66},{3,67},{4,68},{5,69},{6,70},{7,71},{8,12},{9,... | collective-permute-start | bytes 1400840 | tf_op jit(solution)/shard_map/ppermute | solution.py:354
  12.7 4.7 %collective-permute-done.1.first = f32[912,128]{1,0:T(8,128)S(1)} collective-permute-done((f32[912,128]{1,0:T(8,128)S(1)}, f32[912,128]{1,0:T(8,128)S(1)}, u32[]{:S(2)}, u32[]{:S(2)}) %collective-permute-start.1) | collective-permute-done | bytes 466976 | tf_op jit(solution)/shard_map/ppermute | solution.py:354
  17.4 4.6 %collective-permute-done.2.second = f32[912,128]{1,0:T(8,128)S(1)} collective-permute-done((f32[912,128]{1,0:T(8,128)S(1)}, f32[912,128]{1,0:T(8,128)S(1)}, u32[]{:S(2)}, u32[]{:S(2)}) %collective-permute-start.2) | collective-permute-done | bytes 466976 | tf_op jit(solution)/shard_map/ppermute | solution.py:354
  22.0 1.5 %collective-permute-done.3.third = f32[912,128]{1,0:T(8,128)S(1)} collective-permute-done((f32[912,128]{1,0:T(8,128)S(1)}, f32[912,128]{1,0:T(8,128)S(1)}, u32[]{:S(2)}, u32[]{:S(2)}) %collective-permute-start.3) | collective-permute-done | bytes 466976 | tf_op jit(solution)/shard_map/ppermute | solution.py:354
  23.6 0.9 %fold.1 = f32[16,64,128]{2,1,0:T(8,128)} custom-call(f32[912,128]{1,0:T(8,128)S(1)} %collective-permute-done.1.first, f32[912,128]{1,0:T(8,128)S(1)} %collective-permute-done.2.second, f32[912,128]{1,0:T(8,128)S(1)} %collective-permute-done.3.third, f32[912,128]{1,0:T(8,128)S(1)} %get-tuple-element.14.own), custom_call_target="tpu_custom_call" | custom-call | tf_op jit(solution)/shard_map/fold/pallas_call | solution.py:202
  24.5 6.8 %all-to-all-start = ((f32[16,64,128]{2,1,0:T(8,128)}), f32[16,64,128]{2,1,0:T(8,128)S(1)}, u32[]{:S(2)}, u32[]{:S(2)}) async-start(f32[16,64,128]{2,1,0:T(8,128)} %fold.1), calls=%async_computation | async-start | bytes 1048576 | tf_op jit(solution)/shard_map/all_to_all | solution.py:356
  31.2 0.0 copy-done
  31.2 0.0 copy-done.1
  31.3 1.6 %collective-permute-start.4 = (f32[1,3584]{1,0:T(1,128)S(1)}, f32[1,3584]{1,0:T(1,128)S(1)}, u32[]{:S(2)}, u32[]{:S(2)}) collective-permute-start(f32[1,3584]{1,0:T(1,128)S(1)} %broadcast_select_fusion), channel_id=1, source_target_pairs={{0,8},{1,9},{2,10},{3,11},{4,12},{5,13},{6,14},{7,15},{8,0},{9,1},... | collective-permute-start | bytes 43016 | tf_op jit(solution)/shard_map/ppermute | solution.py:54
  32.9 0.8 %collective-permute-done.4.base = f32[1,3584]{1,0:T(1,128)S(1)} collective-permute-done((f32[1,3584]{1,0:T(1,128)S(1)}, f32[1,3584]{1,0:T(1,128)S(1)}, u32[]{:S(2)}, u32[]{:S(2)}) %collective-permute-start.4) | collective-permute-done | bytes 14368 | tf_op jit(solution)/shard_map/ppermute | solution.py:54
  33.7 6.8 %all-to-all-done.blocks = f32[16,64,128]{2,1,0:T(8,128)S(1)} async-done(((f32[16,64,128]{2,1,0:T(8,128)}), f32[16,64,128]{2,1,0:T(8,128)S(1)}, u32[]{:S(2)}, u32[]{:S(2)}) %all-to-all-start) | async-done | bytes 524320 | tf_op jit(solution)/shard_map/all_to_all | solution.py:356
  40.6 0.1 update.1
  40.7 18.9 %all_to_all.10.source = bf16[64,56,128]{2,1,0:T(8,128)(2,1)S(1)} all-to-all(bf16[64,56,128]{2,1,0:T(8,128)(2,1)S(1)} %get-tuple-element.15), channel_id=1, replica_groups={{0,1,2,3,4,5,6,7,16,17,18,19,20,21,22,23,32,33,34,35,36,37,38,39,48,49,..., dimensions={0} | all-to-all | bytes 1835008 | tf_op jit(solution)/shard_map/all_to_all | solution.py:360
  59.6 4.7 %collective-permute-start.5 = (bf16[64,56,128]{2,1,0:T(8,128)(2,1)S(1)}, bf16[64,56,128]{2,1,0:T(8,128)(2,1)S(1)}, u32[]{:S(2)}, u32[]{:S(2)}) collective-permute-start(bf16[64,56,128]{2,1,0:T(8,128)(2,1)S(1)} %all_to_all.10.source), channel_id=1, source_target_pairs={{0,8},{1,9},{2,10},{3,11},{4,12},{5,13},{6,14},{7,15},{8,0},{9,1},... | collective-permute-start | bytes 2752520 | tf_op jit(solution)/shard_map/ppermute | solution.py:54
  64.3 0.0 collective-permute-start.6
  64.3 0.5 lay.1.own_rows
  64.8 1.6 %collective-permute-done.6.other_new = f32[1,3584]{1,0:T(1,128)S(1)} collective-permute-done((f32[1,3584]{1,0:T(1,128)S(1)}, f32[1,3584]{1,0:T(1,128)S(1)}, u32[]{:S(2)}, u32[]{:S(2)}) %collective-permute-start.6) | collective-permute-done | bytes 14368 | tf_op jit(solution)/shard_map/ppermute | solution.py:54
  66.4 0.0 collective-permute-done.5.swapped
  66.4 1.3 %finish.1 = (f32[1,3584]{1,0:T(1,128)}, f32[1,3584]{1,0:T(1,128)}, bf16[128,3584]{1,0:T(8,128)(2,1)}, bf16[128,3584]{1,0:T(8,128)(2,1)}) custom-call(bf16[128,3584]{1,0:T(8,128)(2,1)S(1)} %lay.1.own_rows, bf16[64,56,128]{2,1,0:T(8,128)(2,1)S(1)} %collective-permute-done.5.swapped, f32[1,3584]{1,0:T(1,128)S(1)} %get-tuple-element.16.own_new, ...), custom_call_target="tpu_custom_call" | custom-call | tf_op jit(solution)/shard_map/finish/pallas_call | solution.py:324
  (1 shorter events, 0.0 us)
Async XLA Ops:
  2.3 4.9 %collective-permute-start = (f32[3648,128]{1,0:T(8,128)S(1)}, f32[3648,128]{1,0:T(8,128)S(1)}, u32[]{:S(2)}, u32[]{:S(2)}) collective-permute-start(f32[3648,128]{1,0:T(8,128)S(1)} %weigh_other.1), channel_id=1, source_target_pairs={{0,8},{1,9},{2,10},{3,11},{4,12},{5,13},{6,14},{7,15},{8,0},{9,1},... | collective-permute-start | bytes 5603336 | tf_op jit(solution)/shard_map/ppermute | solution.py:54
  7.5 23.8 %copy-start = (f32[1,3584]{1,0:T(1,128)S(1)}, f32[1,3584]{1,0:T(1,128)}, u32[]{:S(2)}) copy-start(f32[1,3584]{1,0:T(1,128)} %params.1) | copy-start | bytes 43012
  7.5 23.8 %copy-start.1 = (f32[1,3584]{1,0:T(1,128)S(1)}, f32[1,3584]{1,0:T(1,128)}, u32[]{:S(2)}) copy-start(f32[1,3584]{1,0:T(1,128)} %variate.1) | copy-start | bytes 43012
  7.5 9.9 %collective-permute-start.1 = (f32[912,128]{1,0:T(8,128)S(1)}, f32[912,128]{1,0:T(8,128)S(1)}, u32[]{:S(2)}, u32[]{:S(2)}) collective-permute-start(f32[912,128]{1,0:T(8,128)S(1)} %get-tuple-element.11), channel_id=1, source_target_pairs={{0,32},{1,33},{2,34},{3,35},{4,36},{5,37},{6,38},{7,39},{8,10},{9,... | collective-permute-start | bytes 1400840 | tf_op jit(solution)/shard_map/ppermute | solution.py:354
  9.3 12.7 %collective-permute-start.2 = (f32[912,128]{1,0:T(8,128)S(1)}, f32[912,128]{1,0:T(8,128)S(1)}, u32[]{:S(2)}, u32[]{:S(2)}) collective-permute-start(f32[912,128]{1,0:T(8,128)S(1)} %get-tuple-element.12), channel_id=1, source_target_pairs={{0,96},{1,97},{2,98},{3,99},{4,100},{5,101},{6,102},{7,103},{8,14}... | collective-permute-start | bytes 1400840 | tf_op jit(solution)/shard_map/ppermute | solution.py:354
  11.5 12.1 %collective-permute-start.3 = (f32[912,128]{1,0:T(8,128)S(1)}, f32[912,128]{1,0:T(8,128)S(1)}, u32[]{:S(2)}, u32[]{:S(2)}) collective-permute-start(f32[912,128]{1,0:T(8,128)S(1)} %get-tuple-element.13), channel_id=1, source_target_pairs={{0,64},{1,65},{2,66},{3,67},{4,68},{5,69},{6,70},{7,71},{8,12},{9,... | collective-permute-start | bytes 1400840 | tf_op jit(solution)/shard_map/ppermute | solution.py:354
  24.5 16.1 %all-to-all-start = ((f32[16,64,128]{2,1,0:T(8,128)}), f32[16,64,128]{2,1,0:T(8,128)S(1)}, u32[]{:S(2)}, u32[]{:S(2)}) async-start(f32[16,64,128]{2,1,0:T(8,128)} %fold.1), calls=%async_computation | async-start | bytes 1048576 | tf_op jit(solution)/shard_map/all_to_all | solution.py:356
  31.3 2.5 %collective-permute-start.4 = (f32[1,3584]{1,0:T(1,128)S(1)}, f32[1,3584]{1,0:T(1,128)S(1)}, u32[]{:S(2)}, u32[]{:S(2)}) collective-permute-start(f32[1,3584]{1,0:T(1,128)S(1)} %broadcast_select_fusion), channel_id=1, source_target_pairs={{0,8},{1,9},{2,10},{3,11},{4,12},{5,13},{6,14},{7,15},{8,0},{9,1},... | collective-permute-start | bytes 43016 | tf_op jit(solution)/shard_map/ppermute | solution.py:54
  59.6 6.8 %collective-permute-start.5 = (bf16[64,56,128]{2,1,0:T(8,128)(2,1)S(1)}, bf16[64,56,128]{2,1,0:T(8,128)(2,1)S(1)}, u32[]{:S(2)}, u32[]{:S(2)}) collective-permute-start(bf16[64,56,128]{2,1,0:T(8,128)(2,1)S(1)} %all_to_all.10.source), channel_id=1, source_target_pairs={{0,8},{1,9},{2,10},{3,11},{4,12},{5,13},{6,14},{7,15},{8,0},{9,1},... | collective-permute-start | bytes 2752520 | tf_op jit(solution)/shard_map/ppermute | solution.py:54
  64.3 2.1 %collective-permute-start.6 = (f32[1,3584]{1,0:T(1,128)S(1)}, f32[1,3584]{1,0:T(1,128)S(1)}, u32[]{:S(2)}, u32[]{:S(2)}) collective-permute-start(f32[1,3584]{1,0:T(1,128)S(1)} %get-tuple-element.17), channel_id=1, source_target_pairs={{0,8},{1,9},{2,10},{3,11},{4,12},{5,13},{6,14},{7,15},{8,0},{9,1},... | collective-permute-start | bytes 43016 | tf_op jit(solution)/shard_map/ppermute | solution.py:54

commit v4 on v3

--- a/solution.py
+++ b/solution.py
@@ -40,14 +40,21 @@
     return pairs
 
 
+def at(x, y, z, core):
+    return device(2 * x + y // 2, core, 2 * z + y % 2)
+
+
+FOUR = range(4)
+
+
 def plane_groups():
-    groups = [[device(2 * x + h, 0, s) for h in range(2) for s in range(8)] for x in range(4)]
-    groups += [[device(i, 1, 2 * z + low) for low in range(2) for i in range(8)] for z in range(4)]
-    return groups
+    groups = [[at(x, y, z, 0) for y in FOUR for z in FOUR] for x in FOUR]
+    return groups + [[at(x, y, z, 1) for y in FOUR for x in FOUR] for z in FOUR]
 
 
 def chip_groups():
-    return [[device(i, core, s) for i in range(8) for s in range(8)] for core in range(2)]
+    first = [at(x, y, z, 0) for x in FOUR for y in FOUR for z in FOUR]
+    return [first, [at(x, y, z, 1) for z in FOUR for y in FOUR for x in FOUR]]
 
 
 def core_swap(x):
@@ -76,9 +83,17 @@
     return jnp.where(d // 8 % 2 == 0, d // 32, d % 8 // 2)
 
 
+STEPS = (1, 3, 2)
+
+
+def tile_rows(columns):
+    return -(-columns // LANES // 8) * 8
+
+
 def weigh_kernel(
-    other, taking_hbm, counts_hbm, deltas, changes, out, held, taking, counts, arrived, small
+    other, taking_hbm, counts_hbm, deltas, changes, params, variate, out, *scratch
 ):
+    held, taking, counts, row, arrived, small = scratch
     core = my_core()
     owner = 1 - core if other else core
     chunks, pieces = held.shape[0], held.shape[3] // LANES
@@ -121,10 +136,12 @@
     @pl.when(owner == 0)
     def _():
         fetch(deltas)
+        pltpu.make_async_copy(params, row, small.at[2]).start()
 
     @pl.when(owner == 1)
     def _():
         fetch(changes)
+        pltpu.make_async_copy(variate, row, small.at[2]).start()
 
     for copy in scalars:
         copy.wait()
@@ -140,42 +157,52 @@
     def _():
         fill(t0.astype(jnp.float32), t1.astype(jnp.float32), jnp.float32(0), block, group)
 
-
-def weigh(other, taking, counts, deltas, changes):
+    pltpu.make_async_copy(params, row, small.at[2]).wait()
+    for j in range(pieces):
+        out[pl.ds(8 * group + j, 1), :] = row[:, pl.ds(j * LANES, LANES)]
+
+
+def weigh(other, taking, counts, deltas, changes, params, variate):
     rows, columns = deltas.shape[1:]
-    out_rows = 8 * (8 * 2 * columns // LANES + 8)
+    out_rows = 8 * (8 * 2 * columns // LANES + 8) + tile_rows(columns)
     return pl.pallas_call(
         functools.partial(weigh_kernel, other),
-        in_specs=[HBM_SPEC] * 4,
+        in_specs=[HBM_SPEC] * 6,
         out_specs=VMEM_SPEC,
         out_shape=pltpu.VMEM((out_rows, LANES), jnp.float32),
         scratch_shapes=[
             pltpu.VMEM((rows // 16, 2, 16, columns), deltas.dtype),
             pltpu.SMEM(taking.shape, jnp.int32),
             pltpu.SMEM(counts.shape, jnp.int32),
+            pltpu.VMEM(params.shape, jnp.float32),
             pltpu.SemaphoreType.DMA((rows // 16,)),
-            pltpu.SemaphoreType.DMA((2,)),
+            pltpu.SemaphoreType.DMA((3,)),
         ],
         compiler_params=SCOPED,
         name="weigh_other" if other else "weigh_own",
-    )(hbm(taking), hbm(counts), hbm(deltas), hbm(changes))
+    )(*[hbm(a) for a in (taking, counts, deltas, changes, params, variate)])
 
 
 def join_kernel(keep, came, *outs):
-    rows = outs[0].shape[0]
+    *parts, old = outs
+    rows = parts[0].shape[0]
     mine = my_ring()
-    for step, out in zip((1, 3, 2, 0), outs):
+    for step, out in zip((*STEPS, 0), parts):
         at = pl.ds(pl.multiple_of((mine + step) % 4 * rows, 8), rows)
         out[...] = keep[at, :] + came[at, :]
-
-
-def join(keep, came):
-    out = pltpu.VMEM((keep.shape[0] // 4, LANES), jnp.float32)
+    last = pl.ds(4 * rows, old.shape[1])
+    old[0] = keep[last, :]
+    old[1] = came[last, :]
+
+
+def join(keep, came, columns):
+    row = tile_rows(columns)
+    part = pltpu.VMEM(((keep.shape[0] - row) // 4, LANES), jnp.float32)
     return pl.pallas_call(
         join_kernel,
         in_specs=[VMEM_SPEC, VMEM_SPEC],
-        out_specs=[VMEM_SPEC] * 4,
-        out_shape=[out] * 4,
+        out_specs=[VMEM_SPEC] * 5,
+        out_shape=[part] * 4 + [pltpu.VMEM((2, row, LANES), jnp.float32)],
         compiler_params=SCOPED,
         name="join",
     )(vmem(keep), vmem(came))
@@ -184,32 +211,34 @@
 def fold_kernel(first, second, third, own, out):
     group = own.shape[0] // 2
     block = (group - 8) // 8
-
-    def total(at, size):
-        here = pl.ds(at, size)
+    swapped = my_core() == 1
+
+    def total(start, size):
+        here = pl.ds(start, size)
         return own[here, :] + first[here, :] + second[here, :] + third[here, :]
 
+    tail = total(8 * block, 8)
     for g in range(2):
-        tail = total(g * group + 8 * block, 8)
         for b in range(8):
-            out[g * 8 + b, pl.ds(0, block), :] = total(g * group + b * block, block)
-            out[g * 8 + b, pl.ds(block, 8), :] = tail
+            y = jnp.where(swapped, b % 2 * 2 + g, g * 2 + b % 2)
+            start = pl.multiple_of((y * 4 + b // 2) * (block + 8), 8)
+            out[pl.ds(start, block), :] = total(g * group + b * block, block)
+            out[pl.ds(start + block, 8), :] = tail
 
 
 def fold(parts):
-    group = parts[0].shape[0] // 2
-    block = (group - 8) // 8
+    block = (parts[0].shape[0] // 2 - 8) // 8
     return pl.pallas_call(
         fold_kernel,
         in_specs=[VMEM_SPEC] * 4,
         out_specs=VMEM_SPEC,
-        out_shape=pltpu.VMEM((16, block + 8, LANES), jnp.float32),
+        out_shape=pltpu.VMEM((16 * (block + 8), LANES), jnp.float32),
         compiler_params=SCOPED,
         name="fold",
-    )(*[vmem(p) for p in parts])
-
-
-def update_kernel(client_count, blocks, params, variate, base, own, other, spread, total, fresh):
+    )(*[vmem(p) for p in parts]).reshape(16, block + 8, LANES)
+
+
+def update_kernel(client_count, blocks, old, own, other, spread, total, fresh):
     core = my_core()
     count, used = blocks.shape[0], blocks.shape[1] - 8
     pieces = used // 2
@@ -218,39 +247,41 @@
         sums = sums + blocks[k]
     divisor = jnp.where(core == 0, sums[used : used + 1], jnp.float32(client_count))
     total[...] = sums[:used] / divisor
-    for j in range(pieces):
-        lanes = pl.ds(j * LANES, LANES)
-        mine = jnp.where(core == 0, params[:, lanes], variate[:, lanes])
-        mine = mine + total[pl.ds(core * pieces + j, 1), :]
-        theirs = base[:, lanes] + total[pl.ds((1 - core) * pieces + j, 1), :]
-        own[:, lanes] = mine
-        other[:, lanes] = theirs
-        fresh[pl.ds(core * pieces + j, 1), :] = mine
-        fresh[pl.ds((1 - core) * pieces + j, 1), :] = theirs
+    for side, out in ((0, own), (1, other)):
+        start = jnp.where(core == side, 0, pieces)
+        for j in range(pieces):
+            value = old[side, pl.ds(j, 1), :] + total[pl.ds(start + j, 1), :]
+            out[:, pl.ds(j * LANES, LANES)] = value
+            fresh[pl.ds(start + j, 1), :] = value
     rounded = fresh[...].astype(jnp.bfloat16)
     for k in range(CHIPS):
         spread[k] = rounded
 
 
-def update(blocks, params, variate, base, client_count):
+def update(blocks, old, columns, client_count):
     used = blocks.shape[1] - 8
-    row = pltpu.VMEM(params.shape, jnp.float32)
+    row = pltpu.VMEM((1, columns), jnp.float32)
     return pl.pallas_call(
         functools.partial(update_kernel, client_count),
-        in_specs=[VMEM_SPEC] * 4,
+        in_specs=[VMEM_SPEC] * 2,
         out_specs=[VMEM_SPEC] * 3,
         out_shape=[row, row, pltpu.VMEM((CHIPS, used, LANES), jnp.bfloat16)],
         scratch_shapes=[pltpu.VMEM((used, LANES), jnp.float32)] * 2,
         compiler_params=SCOPED,
         name="update",
-    )(vmem(blocks), params, variate, vmem(base))
-
-
-def lay_out(source, wide, put, done=lambda i: None):
-    chips, block = source.shape[:2]
+    )(vmem(blocks), vmem(old))
+
+
+def lay_out(owner, source, wide, put, done=lambda i: None):
+    block = source.shape[1]
     pieces = block // 2
-    for k in range(chips):
-        wide[pl.ds(k * block, block), :] = source[k].astype(jnp.float32)
+    for far in FOUR:
+        for near in FOUR:
+            corner = jnp.where(owner == 0, far * 16 + near * 2, near * 16 + far * 2)
+            for y in FOUR:
+                start = pl.multiple_of((corner + y // 2 * 8 + y % 2) * block, 8)
+                value = source[far * 16 + y * 4 + near]
+                wide[pl.ds(start, block), :] = value.astype(jnp.float32)
 
     def one(i, carry):
         for j in range(pieces):
@@ -267,7 +298,7 @@
         at = pl.ds(pl.multiple_of(i * 16, 16), 16)
         out[at, pl.ds(j * LANES, LANES)] = value
 
-    lay_out(source, wide, put)
+    lay_out(my_core(), source, wide, put)
 
 
 def lay(gathered):
@@ -304,7 +335,7 @@
             at = pl.ds(pl.multiple_of(i * 16, 16), 16)
             return pltpu.make_async_copy(laid.at[at, :], their_rows.at[at, :], sems.at[3 + i])
 
-        lay_out(swapped, wide, put, lambda i: write(i).start())
+        lay_out(1 - core, swapped, wide, put, lambda i: write(i).start())
         for copy in copies:
             copy.wait()
         for i in range(8):
@@ -342,19 +373,17 @@
 
 
 def body(client_deltas, variate_deltas, params, variate, taking_part, counts):
-    first = my_core() == 0
     client_count = 2 * 128
-
-    send = weigh(True, taking_part, counts, client_deltas, variate_deltas)
-    came = core_swap(send)
-    keep = weigh(False, taking_part, counts, client_deltas, variate_deltas)
-    base = core_swap(jnp.where(first, variate, params))
-
-    *quarters, own_quarter = join(keep, came)
-    arrived = [lax.ppermute(vmem(q), AXIS, ring_pairs(k)) for q, k in zip(quarters, (1, 3, 2))]
-    plane = fold([*arrived, own_quarter])
-    blocks = lax.all_to_all(vmem(plane), AXIS, 0, 0, axis_index_groups=plane_groups(), tiled=True)
-    own_new, sent_new, spread = update(blocks, params, variate, base, client_count)
+    columns = params.shape[1]
+    arguments = (taking_part, counts, client_deltas, variate_deltas, params, variate)
+
+    came = core_swap(weigh(True, *arguments))
+    keep = weigh(False, *arguments)
+    *sent, own, old = join(keep, came, columns)
+    sent = [lax.ppermute(vmem(p), AXIS, ring_pairs(k)) for p, k in zip(sent, STEPS)]
+    plane = fold([*sent, own])
+    blocks = lax.all_to_all(plane, AXIS, 0, 0, axis_index_groups=plane_groups(), tiled=True)
+    own_new, sent_new, spread = update(blocks, old, columns, client_count)
 
     other_new = core_swap(sent_new)
     gathered = lax.all_to_all(spread, AXIS, 0, 0, axis_index_groups=chip_groups(), tiled=True)

time: 68 us -> 66.4 us (0.976)
  blocking collectives: 18.9 us -> 34.4 us
  starting transfers between devices: 19.8 us -> 11.2 us
  waiting for transfers between devices: 21.9 us -> 14.2 us
  Pallas kernels: 6.44 us -> 5.7 us
    all_to_all x0 -> x1, blocking collectives: none -> 15.9 us  [body(): lax.all_to_all(plane, AXIS, 0, 0, axis_index_groups=plane_groups(), tiled...]
    all_to_all x1 -> x0, waiting for transfers between devices: 6.84 us -> none  [body(): lax.all_to_all(vmem(plane), AXIS, 0, 0, axis_index_groups=plane_groups(),...]
    all_to_all x1 -> x0, starting transfers between devices: 6.75 us -> none  [body(): lax.all_to_all(vmem(plane), AXIS, 0, 0, axis_index_groups=plane_groups(),...]
    ppermute x4 -> x3, starting transfers between devices: 7.75 us -> 5.94 us  [core_swap(): return lax.ppermute(x, AXIS, swap_pairs())]
    ppermute x4 -> x3, waiting for transfers between devices: 4.21 us -> 3.37 us  [core_swap(): return lax.ppermute(x, AXIS, swap_pairs())]
    pallas_call x1, Pallas kernels: 0.91 us -> 0.12 us  [fold(): pl.pallas_call(fold_kernel, in_specs=[VMEM_SPEC] * 4, out_specs=VMEM_SPEC...]
  transfers between devices with their start and end apart: 8 -> 6, of which waited for: 7 -> 5; matrix products, arithmetic and copies ran while one was open for 0% -> 0% of each run, Pallas kernels for 3% -> 3%
where the time goes in v4:
time: 66.4 us; the launch traced here: 66.1 us
  blocking collectives  34.4 us (52%)
  waiting for transfers between devices  14.2 us (21%)
  starting transfers between devices  11.2 us (17%)
  Pallas kernels  5.7 us (9%)
  between operations  0.67 us (1%)
    all_to_all x1, blocking collectives, body(): lax.all_to_all(spread, AXIS, 0, 0, axis_index_groups=chip_groups(), tiled...  18.5 us
    all_to_all x1, blocking collectives, body(): lax.all_to_all(plane, AXIS, 0, 0, axis_index_groups=plane_groups(), tiled...  15.9 us
    ppermute x3, waiting for transfers between devices, body(): lax.ppermute(vmem(p), AXIS, ring_pairs(k))  10.8 us
    ppermute x3, starting transfers between devices, core_swap(): return lax.ppermute(x, AXIS, swap_pairs())  5.94 us
    ppermute x3, starting transfers between devices, body(): lax.ppermute(vmem(p), AXIS, ring_pairs(k))  5.24 us
    pallas_call x2, Pallas kernels, weigh(): pl.pallas_call(functools.partial(weigh_kernel, other), in_specs=[HBM_SPEC...  3.41 us
    ppermute x3, waiting for transfers between devices, core_swap(): return lax.ppermute(x, AXIS, swap_pairs())  3.37 us
  transfers between devices with their start and end apart: 6, of which 5 were waited for; matrix products, arithmetic and copies ran while one was open for 0% of the time, Pallas kernels for 3%

profile of v4, /device:TPU:1, one launch (start us, length us, event | category | flops | bytes accessed | tf_op | source)
XLA Modules:
  0.0 66.1 jit_solution(15095233809248092913)
XLA Ops:
  0.6 1.7 %weigh_other.1 = f32[3680,128]{1,0:T(8,128)S(1)} custom-call(s32[2]{0:T(128)} %taking_hbm.3, s32[2]{0:T(128)} %counts_hbm.3, bf16[2,128,3584]{2,1,0:T(8,128)(2,1)} %deltas.3, bf16[2,128,3584]{2,1,0:T(8,128)(2,1)} %changes.3, f32[1,3584]{1,0:T(1,128)} %params.3, f32[1,3584]{1,0:T(1,128)} %variate.3), custom_call_target="tpu_custom_call" | custom-call | tf_op jit(solution)/shard_map/weigh_other/pallas_call | solution.py:168
  2.4 1.5 %collective-permute-start = (f32[3680,128]{1,0:T(8,128)S(1)}, f32[3680,128]{1,0:T(8,128)S(1)}, u32[]{:S(2)}, u32[]{:S(2)}) collective-permute-start(f32[3680,128]{1,0:T(8,128)S(1)} %weigh_other.1), channel_id=1, source_target_pairs={{0,8},{1,9},{2,10},{3,11},{4,12},{5,13},{6,14},{7,15},{8,0},{9,1},... | collective-permute-start | bytes 5652488 | tf_op jit(solution)/shard_map/ppermute | solution.py:61
  3.8 1.7 %weigh_own.1.keep = f32[3680,128]{1,0:T(8,128)S(1)} custom-call(s32[2]{0:T(128)} %taking_hbm.3, s32[2]{0:T(128)} %counts_hbm.3, bf16[2,128,3584]{2,1,0:T(8,128)(2,1)} %deltas.3, bf16[2,128,3584]{2,1,0:T(8,128)(2,1)} %changes.3, f32[1,3584]{1,0:T(1,128)} %params.3, f32[1,3584]{1,0:T(1,128)} %variate.3), custom_call_target="tpu_custom_call" | custom-call | tf_op jit(solution)/shard_map/weigh_own/pallas_call | solution.py:168
  5.5 1.8 %collective-permute-done.came = f32[3680,128]{1,0:T(8,128)S(1)} collective-permute-done((f32[3680,128]{1,0:T(8,128)S(1)}, f32[3680,128]{1,0:T(8,128)S(1)}, u32[]{:S(2)}, u32[]{:S(2)}) %collective-permute-start) | collective-permute-done | bytes 1884192 | tf_op jit(solution)/shard_map/ppermute | solution.py:61
  7.3 0.2 join.1
  7.5 1.8 %collective-permute-start.1 = (f32[912,128]{1,0:T(8,128)S(1)}, f32[912,128]{1,0:T(8,128)S(1)}, u32[]{:S(2)}, u32[]{:S(2)}) collective-permute-start(f32[912,128]{1,0:T(8,128)S(1)} %get-tuple-element.12), channel_id=1, source_target_pairs={{0,32},{1,33},{2,34},{3,35},{4,36},{5,37},{6,38},{7,39},{8,10},{9,... | collective-permute-start | bytes 1400840 | tf_op jit(solution)/shard_map/ppermute | solution.py:383
  9.3 2.2 %collective-permute-start.2 = (f32[912,128]{1,0:T(8,128)S(1)}, f32[912,128]{1,0:T(8,128)S(1)}, u32[]{:S(2)}, u32[]{:S(2)}) collective-permute-start(f32[912,128]{1,0:T(8,128)S(1)} %get-tuple-element.13), channel_id=1, source_target_pairs={{0,96},{1,97},{2,98},{3,99},{4,100},{5,101},{6,102},{7,103},{8,14}... | collective-permute-start | bytes 1400840 | tf_op jit(solution)/shard_map/ppermute | solution.py:383
  11.5 1.2 %collective-permute-start.3 = (f32[912,128]{1,0:T(8,128)S(1)}, f32[912,128]{1,0:T(8,128)S(1)}, u32[]{:S(2)}, u32[]{:S(2)}) collective-permute-start(f32[912,128]{1,0:T(8,128)S(1)} %get-tuple-element.14), channel_id=1, source_target_pairs={{0,64},{1,65},{2,66},{3,67},{4,68},{5,69},{6,70},{7,71},{8,12},{9,... | collective-permute-start | bytes 1400840 | tf_op jit(solution)/shard_map/ppermute | solution.py:383
  12.7 4.7 %collective-permute-done.1.first = f32[912,128]{1,0:T(8,128)S(1)} collective-permute-done((f32[912,128]{1,0:T(8,128)S(1)}, f32[912,128]{1,0:T(8,128)S(1)}, u32[]{:S(2)}, u32[]{:S(2)}) %collective-permute-start.1) | collective-permute-done | bytes 466976 | tf_op jit(solution)/shard_map/ppermute | solution.py:383
  17.4 4.6 %collective-permute-done.2.second = f32[912,128]{1,0:T(8,128)S(1)} collective-permute-done((f32[912,128]{1,0:T(8,128)S(1)}, f32[912,128]{1,0:T(8,128)S(1)}, u32[]{:S(2)}, u32[]{:S(2)}) %collective-permute-start.2) | collective-permute-done | bytes 466976 | tf_op jit(solution)/shard_map/ppermute | solution.py:383
  22.0 1.5 %collective-permute-done.3.third = f32[912,128]{1,0:T(8,128)S(1)} collective-permute-done((f32[912,128]{1,0:T(8,128)S(1)}, f32[912,128]{1,0:T(8,128)S(1)}, u32[]{:S(2)}, u32[]{:S(2)}) %collective-permute-start.3) | collective-permute-done | bytes 466976 | tf_op jit(solution)/shard_map/ppermute | solution.py:383
  23.6 0.1 fold.1
  23.7 15.9 %all_to_all.10.blocks = f32[16,64,128]{2,1,0:T(8,128)S(1)} all-to-all(f32[16,64,128]{2,1,0:T(8,128)S(1)} %bitcast.1), channel_id=1, replica_groups={{0,2,4,6,1,3,5,7,16,18,20,22,17,19,21,23},{32,34,36,38,33,35,37,39,48,5..., dimensions={0} | all-to-all | bytes 1048576 | tf_op jit(solution)/shard_map/all_to_all | solution.py:385
  39.6 0.1 update.1
  39.7 18.5 %all_to_all.11.source = bf16[64,56,128]{2,1,0:T(8,128)(2,1)S(1)} all-to-all(bf16[64,56,128]{2,1,0:T(8,128)(2,1)S(1)} %get-tuple-element.17), channel_id=1, replica_groups={{0,2,4,6,1,3,5,7,16,18,20,22,17,19,21,23,32,34,36,38,33,35,37,39,48,50,..., dimensions={0} | all-to-all | bytes 1835008 | tf_op jit(solution)/shard_map/all_to_all | solution.py:389
  58.2 4.5 %collective-permute-start.4 = (bf16[64,56,128]{2,1,0:T(8,128)(2,1)S(1)}, bf16[64,56,128]{2,1,0:T(8,128)(2,1)S(1)}, u32[]{:S(2)}, u32[]{:S(2)}) collective-permute-start(bf16[64,56,128]{2,1,0:T(8,128)(2,1)S(1)} %all_to_all.11.source), channel_id=1, source_target_pairs={{0,8},{1,9},{2,10},{3,11},{4,12},{5,13},{6,14},{7,15},{8,0},{9,1},... | collective-permute-start | bytes 2752520 | tf_op jit(solution)/shard_map/ppermute | solution.py:61
  62.7 0.0 collective-permute-start.5
  62.7 0.5 lay.1.own_rows
  63.2 1.6 %collective-permute-done.5.other_new = f32[1,3584]{1,0:T(1,128)S(1)} collective-permute-done((f32[1,3584]{1,0:T(1,128)S(1)}, f32[1,3584]{1,0:T(1,128)S(1)}, u32[]{:S(2)}, u32[]{:S(2)}) %collective-permute-start.5) | collective-permute-done | bytes 14368 | tf_op jit(solution)/shard_map/ppermute | solution.py:61
  64.8 0.0 collective-permute-done.4.swapped
  64.8 1.3 %finish.1 = (f32[1,3584]{1,0:T(1,128)}, f32[1,3584]{1,0:T(1,128)}, bf16[128,3584]{1,0:T(8,128)(2,1)}, bf16[128,3584]{1,0:T(8,128)(2,1)}) custom-call(bf16[128,3584]{1,0:T(8,128)(2,1)S(1)} %lay.1.own_rows, bf16[64,56,128]{2,1,0:T(8,128)(2,1)S(1)} %collective-permute-done.4.swapped, f32[1,3584]{1,0:T(1,128)S(1)} %get-tuple-element.18.own_new, ...), custom_call_target="tpu_custom_call" | custom-call | tf_op jit(solution)/shard_map/finish/pallas_call | solution.py:355
Async XLA Ops:
  2.4 4.9 %collective-permute-start = (f32[3680,128]{1,0:T(8,128)S(1)}, f32[3680,128]{1,0:T(8,128)S(1)}, u32[]{:S(2)}, u32[]{:S(2)}) collective-permute-start(f32[3680,128]{1,0:T(8,128)S(1)} %weigh_other.1), channel_id=1, source_target_pairs={{0,8},{1,9},{2,10},{3,11},{4,12},{5,13},{6,14},{7,15},{8,0},{9,1},... | collective-permute-start | bytes 5652488 | tf_op jit(solution)/shard_map/ppermute | solution.py:61
  7.5 9.9 %collective-permute-start.1 = (f32[912,128]{1,0:T(8,128)S(1)}, f32[912,128]{1,0:T(8,128)S(1)}, u32[]{:S(2)}, u32[]{:S(2)}) collective-permute-start(f32[912,128]{1,0:T(8,128)S(1)} %get-tuple-element.12), channel_id=1, source_target_pairs={{0,32},{1,33},{2,34},{3,35},{4,36},{5,37},{6,38},{7,39},{8,10},{9,... | collective-permute-start | bytes 1400840 | tf_op jit(solution)/shard_map/ppermute | solution.py:383
  9.3 12.7 %collective-permute-start.2 = (f32[912,128]{1,0:T(8,128)S(1)}, f32[912,128]{1,0:T(8,128)S(1)}, u32[]{:S(2)}, u32[]{:S(2)}) collective-permute-start(f32[912,128]{1,0:T(8,128)S(1)} %get-tuple-element.13), channel_id=1, source_target_pairs={{0,96},{1,97},{2,98},{3,99},{4,100},{5,101},{6,102},{7,103},{8,14}... | collective-permute-start | bytes 1400840 | tf_op jit(solution)/shard_map/ppermute | solution.py:383
  11.5 12.1 %collective-permute-start.3 = (f32[912,128]{1,0:T(8,128)S(1)}, f32[912,128]{1,0:T(8,128)S(1)}, u32[]{:S(2)}, u32[]{:S(2)}) collective-permute-start(f32[912,128]{1,0:T(8,128)S(1)} %get-tuple-element.14), channel_id=1, source_target_pairs={{0,64},{1,65},{2,66},{3,67},{4,68},{5,69},{6,70},{7,71},{8,12},{9,... | collective-permute-start | bytes 1400840 | tf_op jit(solution)/shard_map/ppermute | solution.py:383
  58.2 6.6 %collective-permute-start.4 = (bf16[64,56,128]{2,1,0:T(8,128)(2,1)S(1)}, bf16[64,56,128]{2,1,0:T(8,128)(2,1)S(1)}, u32[]{:S(2)}, u32[]{:S(2)}) collective-permute-start(bf16[64,56,128]{2,1,0:T(8,128)(2,1)S(1)} %all_to_all.11.source), channel_id=1, source_target_pairs={{0,8},{1,9},{2,10},{3,11},{4,12},{5,13},{6,14},{7,15},{8,0},{9,1},... | collective-permute-start | bytes 2752520 | tf_op jit(solution)/shard_map/ppermute | solution.py:61
  62.7 2.1 %collective-permute-start.5 = (f32[1,3584]{1,0:T(1,128)S(1)}, f32[1,3584]{1,0:T(1,128)S(1)}, u32[]{:S(2)}, u32[]{:S(2)}) collective-permute-start(f32[1,3584]{1,0:T(1,128)S(1)} %get-tuple-element.19), channel_id=1, source_target_pairs={{0,8},{1,9},{2,10},{3,11},{4,12},{5,13},{6,14},{7,15},{8,0},{9,1},... | collective-permute-start | bytes 43016 | tf_op jit(solution)/shard_map/ppermute | solution.py:61
